TPU v7x, 32 devices: a whole 2x2x4 slice. The times are simulated.
32 devices in a mesh: fsdp: 16 (over z, y, core), seq: 2 (over x).
Axes of the slice: x: 2, y: 2, z: 4, core: 2. Of those that a mesh axis runs over, the one named last changes fastest.
Arguments:
- tokens_in: bfloat16 [16, 512, 768], P('fsdp', 'seq'), may hold values from -6 to 6
- patches: bfloat16 [16, 2048, 768], P('fsdp', 'seq'), may hold values from -6 to 6
- segment_ids: int32 [16, 512], P('fsdp'), may hold values from 0 to 15, never falling along the last dimension, each value on 1 to 64 neighbouring positions
- key_valid: int32 [16, 512], P('fsdp'), may hold values 0 or 1
- out_grad: bfloat16 [16, 512, 768], P('fsdp', 'seq'), may hold values from -6 to 6
- self_gain: bfloat16 [768], P('fsdp'), may hold values from 0.5 to 1.5
- self_query: bfloat16 [768, 768], P('fsdp'), may hold values from -0.21875 to 0.21875
- self_key: bfloat16 [768, 768], P('fsdp'), may hold values from -0.21875 to 0.21875
- self_value: bfloat16 [768, 768], P('fsdp'), may hold values from -0.21875 to 0.21875
- self_output: bfloat16 [768, 768], P('fsdp'), may hold values from -0.875 to 0.875
- cross_gain: bfloat16 [768], P('fsdp'), may hold values from 0.5 to 1.5
- cross_query: bfloat16 [768, 768], P('fsdp'), may hold values from -0.21875 to 0.21875
- cross_key: bfloat16 [768, 768], P('fsdp'), may hold values from -0.21875 to 0.21875
- cross_value: bfloat16 [768, 768], P('fsdp'), may hold values from -0.21875 to 0.21875
- cross_output: bfloat16 [768, 768], P('fsdp'), may hold values from -2.5 to 2.5
- mlp_gain: bfloat16 [768], P('fsdp'), may hold values from 0.5 to 1.5
- mlp_gate: bfloat16 [768, 2048], P('fsdp'), may hold values from -0.21875 to 0.21875
- mlp_up: bfloat16 [768, 2048], P('fsdp'), may hold values from -0.21875 to 0.21875
- mlp_down: bfloat16 [2048, 768], P('fsdp'), may hold values from -0.125 to 0.125
Outputs:
- layer_out: bfloat16 [16, 512, 768], P('fsdp', 'seq')
- input_grad: float32 [16, 512, 768], P('fsdp', 'seq')
- patch_grad: float32 [16, 2048, 768], P('fsdp', 'seq')
- self_gain_grad: float32 [768], P('fsdp')
- self_query_grad: float32 [768, 768], P('fsdp')
- self_key_grad: float32 [768, 768], P('fsdp')
- self_value_grad: float32 [768, 768], P('fsdp')
- self_output_grad: float32 [768, 768], P('fsdp')
- cross_gain_grad: float32 [768], P('fsdp')
- cross_query_grad: float32 [768, 768], P('fsdp')
- cross_key_grad: float32 [768, 768], P('fsdp')
- cross_value_grad: float32 [768, 768], P('fsdp')
- cross_output_grad: float32 [768, 768], P('fsdp')
- mlp_gain_grad: float32 [768], P('fsdp')
- mlp_gate_grad: float32 [768, 2048], P('fsdp')
- mlp_up_grad: float32 [768, 2048], P('fsdp')
- mlp_down_grad: float32 [2048, 768], P('fsdp')
Inputs may be any that keep to these rules, and one draw needn't show every extreme that they name: `segment_ids`: along an item's row the answer number never falls; every answer has 1 to 64 tokens.
All inputs are finite; a program needn't handle non-finite values. No bound on the sum of `key_valid` on one device may be relied on, other than what follows from the above.
Results may differ from a plain program's by a relative error of at most 0.023.
Values may be sent and summed in bfloat16 or wider, within the bound.
No kernel may reach another device: no remote copies, remote signals or barrier semaphores. Data moves between devices by JAX's collectives and lax.ppermute only.
A program may use at most 192 MiB of HBM per device.

v0:
```python
import jax
import jax.numpy as jnp
from jax import lax
from jax.sharding import PartitionSpec as P

H = 12


EPSILON = 1e-06
SCORE_SCALE = 0.125
MASKED = -1e30


def normalize(tensor, scale_vec):
    return (
        tensor * lax.rsqrt(jnp.mean(tensor * tensor, axis=-1, keepdims=True) + EPSILON) * scale_vec
    )


def activate(gate_pre, up_pre):
    return jax.nn.gelu(gate_pre, approximate=True) * up_pre


def project(activation, matrix):
    return jnp.dot(activation, matrix, preferred_element_type=jnp.float32)


def project_back(gradient, matrix):
    return lax.dot_general(
        gradient, matrix, (((1,), (1,)), ((), ())), preferred_element_type=jnp.float32
    )


def weight_gradient(activation, gradient):
    return lax.dot_general(
        activation, gradient, (((0,), (0,)), ((), ())), preferred_element_type=jnp.float32
    )


def split_heads(tensor, item_count):
    seq_rows = tensor.shape[0] // item_count
    return tensor.reshape(item_count, seq_rows, H, -1).transpose(2, 0, 1, 3)


def join_items(tensor):
    head_count, item_count, seq_rows, head_width = tensor.shape
    return tensor.transpose(1, 2, 0, 3).reshape(item_count, seq_rows, head_count * head_width)


def join_rows(tensor):
    joined = join_items(tensor)
    return joined.reshape(joined.shape[0] * joined.shape[1], joined.shape[2])


def score_block(head_q, head_key_rows, allowed):
    scores = SCORE_SCALE * jnp.einsum(
        "iqd,ikd->iqk", head_q, head_key_rows, preferred_element_type=jnp.float32
    )
    if allowed is None:
        return scores
    return jnp.where(allowed, scores, MASKED)


def attend_forward(query_rows, keys_all, values_all, allowed):

    def one_head(operands):
        head_q, head_key_rows, head_v = operands
        scores = score_block(head_q, head_key_rows, allowed)
        highest = jnp.max(scores, axis=-1, keepdims=True)
        log_total = highest + jnp.log(jnp.sum(jnp.exp(scores - highest), axis=-1, keepdims=True))
        weights = jnp.exp(scores - log_total).astype(jnp.bfloat16)
        mixed = jnp.einsum("iqk,ikd->iqd", weights, head_v, preferred_element_type=jnp.float32)
        return (mixed.astype(jnp.bfloat16), log_total)

    return lax.map(one_head, (query_rows, keys_all, values_all))


def attend_backward(query_rows, keys_all, values_all, allowed, log_totals, grad_mixed):

    def one_head(operands):
        head_q, head_key_rows, head_v, log_total, head_grad = operands
        weights = jnp.exp(score_block(head_q, head_key_rows, allowed) - log_total)
        grad_weights = jnp.einsum(
            "iqd,ikd->iqk", head_grad, head_v, preferred_element_type=jnp.float32
        )
        carried = jnp.sum(weights * grad_weights, axis=-1, keepdims=True)
        grad_scores = (weights * (grad_weights - carried)).astype(jnp.bfloat16)
        grad_q = SCORE_SCALE * jnp.einsum(
            "iqk,ikd->iqd", grad_scores, head_key_rows, preferred_element_type=jnp.float32
        )
        grad_k = SCORE_SCALE * jnp.einsum(
            "iqk,iqd->ikd", grad_scores, head_q, preferred_element_type=jnp.float32
        )
        grad_v = jnp.einsum(
            "iqk,iqd->ikd",
            weights.astype(jnp.bfloat16),
            head_grad,
            preferred_element_type=jnp.float32,
        )
        return (grad_q, grad_k, grad_v)

    return lax.map(one_head, (query_rows, keys_all, values_all, log_totals, grad_mixed))


def gather_self(self_gain, self_query, self_key, self_value, self_output):
    return (
        lax.all_gather(self_gain, "fsdp", axis=0, tiled=True),
        lax.all_gather(self_query, "fsdp", axis=0, tiled=True),
        lax.all_gather(self_key, "fsdp", axis=0, tiled=True),
        lax.all_gather(self_value, "fsdp", axis=0, tiled=True),
        lax.all_gather(self_output, "fsdp", axis=0, tiled=True),
    )


def gather_cross(cross_gain, cross_query, cross_key, cross_value, cross_output):
    return (
        lax.all_gather(cross_gain, "fsdp", axis=0, tiled=True),
        lax.all_gather(cross_query, "fsdp", axis=0, tiled=True),
        lax.all_gather(cross_key, "fsdp", axis=0, tiled=True),
        lax.all_gather(cross_value, "fsdp", axis=0, tiled=True),
        lax.all_gather(cross_output, "fsdp", axis=0, tiled=True),
    )


def gather_mlp(mlp_gain, mlp_gate, mlp_up, mlp_down):
    return (
        lax.all_gather(mlp_gain, "fsdp", axis=0, tiled=True),
        lax.all_gather(mlp_gate, "fsdp", axis=0, tiled=True),
        lax.all_gather(mlp_up, "fsdp", axis=0, tiled=True),
        lax.all_gather(mlp_down, "fsdp", axis=0, tiled=True),
    )


def local(
    tokens_in,
    patches,
    segment_ids,
    key_valid,
    out_grad,
    self_gain,
    self_query,
    self_key,
    self_value,
    self_output,
    cross_gain,
    cross_query,
    cross_key,
    cross_value,
    cross_output,
    mlp_gain,
    mlp_gate,
    mlp_up,
    mlp_down,
):
    item_count, tok_local, feature_dim = tokens_in.shape
    patch_local = patches.shape[1]
    tok_total = segment_ids.shape[1]
    row_count = item_count * tok_local
    seq_start = lax.axis_index("seq") * tok_local
    query_pos = seq_start + jnp.arange(tok_local, dtype=jnp.int32)
    key_pos = jnp.arange(tok_total, dtype=jnp.int32)
    query_seg = lax.dynamic_slice_in_dim(segment_ids, seq_start, tok_local, 1)
    same_seg = query_seg[:, :, None] == segment_ids[:, None, :]
    causal = key_pos[None, None, :] <= query_pos[None, :, None]
    own_key = key_pos[None, None, :] == query_pos[None, :, None]
    allowed = same_seg & causal & ((key_valid[:, None, :] == 1) | own_key)
    flat_in = tokens_in.reshape(row_count, feature_dim).astype(jnp.float32)
    flat_patch = patches.reshape(item_count * patch_local, feature_dim)
    gain_one, w_query, w_key, w_value, w_output = gather_self(
        self_gain, self_query, self_key, self_value, self_output
    )
    first_normed_input = normalize(flat_in, gain_one.astype(jnp.float32)).astype(jnp.bfloat16)
    query_one = project(first_normed_input, w_query).astype(jnp.bfloat16)
    key_one = (
        project(first_normed_input, w_key).astype(jnp.bfloat16).reshape(item_count, tok_local, -1)
    )
    value_one = (
        project(first_normed_input, w_value).astype(jnp.bfloat16).reshape(item_count, tok_local, -1)
    )
    keys_one, values_one = (
        lax.all_gather(key_one, "seq", axis=1, tiled=True),
        lax.all_gather(value_one, "seq", axis=1, tiled=True),
    )
    heads_query_one = split_heads(query_one, item_count)
    heads_key_one = split_heads(keys_one.reshape(item_count * tok_total, -1), item_count)
    heads_value_one = split_heads(values_one.reshape(item_count * tok_total, -1), item_count)
    mixed_one, totals_one = attend_forward(heads_query_one, heads_key_one, heads_value_one, allowed)
    attn_one = join_rows(mixed_one)
    hidden_one = flat_in + project(attn_one, w_output)
    gain_two, c_query, c_key, c_value, c_output = gather_cross(
        cross_gain, cross_query, cross_key, cross_value, cross_output
    )
    normed_two = normalize(hidden_one, gain_two.astype(jnp.float32)).astype(jnp.bfloat16)
    query_two = project(normed_two, c_query).astype(jnp.bfloat16)
    key_part = project(flat_patch, c_key).astype(jnp.bfloat16).reshape(item_count, patch_local, -1)
    value_part = (
        project(flat_patch, c_value).astype(jnp.bfloat16).reshape(item_count, patch_local, -1)
    )
    keys_full, values_full = (
        lax.all_gather(key_part, "seq", axis=1, tiled=True),
        lax.all_gather(value_part, "seq", axis=1, tiled=True),
    )
    heads_query_two = split_heads(query_two, item_count)
    heads_key_two = split_heads(keys_full.reshape(-1, keys_full.shape[2]), item_count)
    heads_value_two = split_heads(values_full.reshape(-1, values_full.shape[2]), item_count)
    mixed_two, totals_two = attend_forward(heads_query_two, heads_key_two, heads_value_two, None)
    attn_two = join_rows(mixed_two)
    hidden_two = hidden_one + project(attn_two, c_output)
    gain_three, m_gate, m_up, m_down = gather_mlp(mlp_gain, mlp_gate, mlp_up, mlp_down)
    normed_three = normalize(hidden_two, gain_three.astype(jnp.float32)).astype(jnp.bfloat16)
    gate_pre = project(normed_three, m_gate)
    up_pre = project(normed_three, m_up)
    inner_act = activate(gate_pre, up_pre).astype(jnp.bfloat16)
    layer_out = (hidden_two + project(inner_act, m_down)).astype(jnp.bfloat16)
    layer_out = layer_out.reshape(item_count, tok_local, feature_dim)
    grad_top = out_grad.reshape(row_count, feature_dim)
    gain_three, m_gate, m_up, m_down = gather_mlp(mlp_gain, mlp_gate, mlp_up, mlp_down)
    grad_mdown = weight_gradient(inner_act, grad_top)
    grad_inner = project_back(grad_top, m_down)
    ignored, act_pull = jax.vjp(activate, gate_pre, up_pre)
    grad_gate, grad_up = act_pull(grad_inner)
    grad_gate = grad_gate.astype(jnp.bfloat16)
    grad_up = grad_up.astype(jnp.bfloat16)
    grad_mgate = weight_gradient(normed_three, grad_gate)
    grad_mup = weight_gradient(normed_three, grad_up)
    grad_normed = project_back(grad_gate, m_gate) + project_back(grad_up, m_up)
    ignored, norm_pull = jax.vjp(normalize, hidden_two, gain_three.astype(jnp.float32))
    grad_hidden, grad_gthree = norm_pull(grad_normed)
    grad_after = grad_top.astype(jnp.float32) + grad_hidden
    gain_two, c_query, c_key, c_value, c_output = gather_cross(
        cross_gain, cross_query, cross_key, cross_value, cross_output
    )
    grad_cross_in = grad_after.astype(jnp.bfloat16)
    grad_coutput = weight_gradient(attn_two, grad_cross_in)
    grad_attn_two = project_back(grad_cross_in, c_output).astype(jnp.bfloat16)
    grad_qh, grad_kh, grad_vh = attend_backward(
        heads_query_two,
        heads_key_two,
        heads_value_two,
        None,
        totals_two,
        split_heads(grad_attn_two, item_count),
    )
    grad_query_two = join_rows(grad_qh).astype(jnp.bfloat16)
    grad_key_mine, grad_value_mine = (
        lax.psum_scatter(
            join_items(grad_kh).astype(jnp.bfloat16), "seq", scatter_dimension=1, tiled=True
        ).astype(jnp.float32),
        lax.psum_scatter(
            join_items(grad_vh).astype(jnp.bfloat16), "seq", scatter_dimension=1, tiled=True
        ).astype(jnp.float32),
    )
    grad_key_two = grad_key_mine.reshape(item_count * patch_local, -1).astype(jnp.bfloat16)
    grad_value_two = grad_value_mine.reshape(item_count * patch_local, -1).astype(jnp.bfloat16)
    grad_ckey = weight_gradient(flat_patch, grad_key_two)
    grad_cvalue = weight_gradient(flat_patch, grad_value_two)
    patch_grad = project_back(grad_key_two, c_key) + project_back(grad_value_two, c_value)
    patch_grad = patch_grad.reshape(item_count, patch_local, feature_dim)
    grad_cquery = weight_gradient(normed_two, grad_query_two)
    ignored, norm_pull = jax.vjp(normalize, hidden_one, gain_two.astype(jnp.float32))
    grad_hidden, grad_gtwo = norm_pull(project_back(grad_query_two, c_query))
    grad_middle = grad_after + grad_hidden
    gain_one, w_query, w_key, w_value, w_output = gather_self(
        self_gain, self_query, self_key, self_value, self_output
    )
    grad_self_in = grad_middle.astype(jnp.bfloat16)
    grad_soutput = weight_gradient(attn_one, grad_self_in)
    grad_attn_one = project_back(grad_self_in, w_output).astype(jnp.bfloat16)
    grad_qh, grad_kh, grad_vh = attend_backward(
        heads_query_one,
        heads_key_one,
        heads_value_one,
        allowed,
        totals_one,
        split_heads(grad_attn_one, item_count),
    )
    grad_query_one = join_rows(grad_qh).astype(jnp.bfloat16)
    grad_key_mine, grad_value_mine = (
        lax.psum_scatter(
            join_items(grad_kh).astype(jnp.bfloat16), "seq", scatter_dimension=1, tiled=True
        ).astype(jnp.float32),
        lax.psum_scatter(
            join_items(grad_vh).astype(jnp.bfloat16), "seq", scatter_dimension=1, tiled=True
        ).astype(jnp.float32),
    )
    first_key_gradient = grad_key_mine.reshape(row_count, -1).astype(jnp.bfloat16)
    grad_value_one = grad_value_mine.reshape(row_count, -1).astype(jnp.bfloat16)
    grad_squery = weight_gradient(first_normed_input, grad_query_one)
    self_key_gradient = weight_gradient(first_normed_input, first_key_gradient)
    grad_svalue = weight_gradient(first_normed_input, grad_value_one)
    grad_normed_one = (
        project_back(grad_query_one, w_query)
        + project_back(first_key_gradient, w_key)
        + project_back(grad_value_one, w_value)
    )
    ignored, norm_pull = jax.vjp(normalize, flat_in, gain_one.astype(jnp.float32))
    grad_hidden, grad_gone = norm_pull(grad_normed_one)
    input_grad = (grad_middle + grad_hidden).reshape(item_count, tok_local, feature_dim)
    all_grads = (
        grad_gone,
        grad_squery,
        self_key_gradient,
        grad_svalue,
        grad_soutput,
        grad_gtwo,
        grad_cquery,
        grad_ckey,
        grad_cvalue,
        grad_coutput,
        grad_gthree,
        grad_mgate,
        grad_mup,
        grad_mdown,
    )
    shares = (
        lax.psum_scatter(all_grads[0], "fsdp", scatter_dimension=0, tiled=True),
        lax.psum_scatter(all_grads[1], "fsdp", scatter_dimension=0, tiled=True),
        lax.psum_scatter(all_grads[2], "fsdp", scatter_dimension=0, tiled=True),
        lax.psum_scatter(all_grads[3], "fsdp", scatter_dimension=0, tiled=True),
        lax.psum_scatter(all_grads[4], "fsdp", scatter_dimension=0, tiled=True),
        lax.psum_scatter(all_grads[5], "fsdp", scatter_dimension=0, tiled=True),
        lax.psum_scatter(all_grads[6], "fsdp", scatter_dimension=0, tiled=True),
        lax.psum_scatter(all_grads[7], "fsdp", scatter_dimension=0, tiled=True),
        lax.psum_scatter(all_grads[8], "fsdp", scatter_dimension=0, tiled=True),
        lax.psum_scatter(all_grads[9], "fsdp", scatter_dimension=0, tiled=True),
        lax.psum_scatter(all_grads[10], "fsdp", scatter_dimension=0, tiled=True),
        lax.psum_scatter(all_grads[11], "fsdp", scatter_dimension=0, tiled=True),
        lax.psum_scatter(all_grads[12], "fsdp", scatter_dimension=0, tiled=True),
        lax.psum_scatter(all_grads[13], "fsdp", scatter_dimension=0, tiled=True),
    )
    owned = (
        lax.psum(shares[0].astype(jnp.bfloat16), "seq").astype(jnp.float32),
        lax.psum(shares[1].astype(jnp.bfloat16), "seq").astype(jnp.float32),
        lax.psum(shares[2].astype(jnp.bfloat16), "seq").astype(jnp.float32),
        lax.psum(shares[3].astype(jnp.bfloat16), "seq").astype(jnp.float32),
        lax.psum(shares[4].astype(jnp.bfloat16), "seq").astype(jnp.float32),
        lax.psum(shares[5].astype(jnp.bfloat16), "seq").astype(jnp.float32),
        lax.psum(shares[6].astype(jnp.bfloat16), "seq").astype(jnp.float32),
        lax.psum(shares[7].astype(jnp.bfloat16), "seq").astype(jnp.float32),
        lax.psum(shares[8].astype(jnp.bfloat16), "seq").astype(jnp.float32),
        lax.psum(shares[9].astype(jnp.bfloat16), "seq").astype(jnp.float32),
        lax.psum(shares[10].astype(jnp.bfloat16), "seq").astype(jnp.float32),
        lax.psum(shares[11].astype(jnp.bfloat16), "seq").astype(jnp.float32),
        lax.psum(shares[12].astype(jnp.bfloat16), "seq").astype(jnp.float32),
        lax.psum(shares[13].astype(jnp.bfloat16), "seq").astype(jnp.float32),
    )
    return (
        layer_out,
        input_grad,
        patch_grad,
        owned[0],
        owned[1],
        owned[2],
        owned[3],
        owned[4],
        owned[5],
        owned[6],
        owned[7],
        owned[8],
        owned[9],
        owned[10],
        owned[11],
        owned[12],
        owned[13],
    )


def solution(mesh):
    in_specs = (
        P("fsdp", "seq", None),
        P("fsdp", "seq", None),
        P("fsdp", None),
        P("fsdp", None),
        P("fsdp", "seq", None),
        P("fsdp"),
        P("fsdp", None),
        P("fsdp", None),
        P("fsdp", None),
        P("fsdp", None),
        P("fsdp"),
        P("fsdp", None),
        P("fsdp", None),
        P("fsdp", None),
        P("fsdp", None),
        P("fsdp"),
        P("fsdp", None),
        P("fsdp", None),
        P("fsdp", None),
    )
    out_specs = (
        P("fsdp", "seq", None),
        P("fsdp", "seq", None),
        P("fsdp", "seq", None),
        P("fsdp"),
        P("fsdp", None),
        P("fsdp", None),
        P("fsdp", None),
        P("fsdp", None),
        P("fsdp"),
        P("fsdp", None),
        P("fsdp", None),
        P("fsdp", None),
        P("fsdp", None),
        P("fsdp"),
        P("fsdp", None),
        P("fsdp", None),
        P("fsdp", None),
    )
    return jax.shard_map(local, mesh=mesh, in_specs=in_specs, out_specs=out_specs, check_vma=False)
```

profile of v0, /device:TPU:0, one launch (start us, length us, event | category | flops | bytes accessed | tf_op | source)
XLA Modules:
  0.0 1808.7 jit_solution(17504396874675185043)
XLA Ops:
  12.0 39.4 %all-gather.28.cloned.1.call-done = bf16[768,768]{1,0:T(8,128)(2,1)} async-done(((bf16[48,768]{1,0:T(8,128)(2,1)}), bf16[768,768]{1,0:T(8,128)(2,1)}) %all-gather.28.cloned.1.call-update) | async-done | bytes 1179664 | tf_op jit(solution)/shard_map/all_gather | solution.py:119
  51.4 3.8 convolution_convert_fusion.3
  55.2 35.6 %all-gather.30.cloned.1.call-done = bf16[768,768]{1,0:T(8,128)(2,1)} async-done(((bf16[48,768]{1,0:T(8,128)(2,1)}), bf16[768,768]{1,0:T(8,128)(2,1)}) %all-gather.30.cloned.1.call-update) | async-done | bytes 1179664 | tf_op jit(solution)/shard_map/all_gather | solution.py:120
  90.8 3.9 convolution_convert_fusion.2
  100.0 32.4 %all-reduce.7 = (bf16[768]{0:T(1024)(128)(2,1)S(1)}, bf16[768]{0:T(1024)(128)(2,1)S(1)}, bf16[768]{0:T(1024)(128)(2,1)S(1)}) all-reduce(bf16[768]{0:T(1024)(128)(2,1)S(1)} %dynamic-update-slice, bf16[768]{0:T(1024)(128)(2,1)S(1)} %dynamic-update-slice.1, bf16[768]{0:T(1024)(128)(2,1)S(1)} %dynamic-update-slice.2), channel_id=1, replica_groups=mesh['fsdp'=16,'seq'=2] {'fsdp'}, use_global_device_ids=true, to_apply=%add | all-reduce | flops 2304 | bytes 9216
  136.8 33.1 %all-gather.20.cloned.1.call-done = bf16[768,768]{1,0:T(8,128)(2,1)} async-done(((bf16[48,768]{1,0:T(8,128)(2,1)}), bf16[768,768]{1,0:T(8,128)(2,1)}) %all-gather.20.cloned.1.call-update) | async-done | bytes 1179664 | tf_op jit(solution)/shard_map/all_gather | solution.py:109
  171.8 11.9 all-gather
  185.5 23.7 %all-gather.22.cloned.1.call-done = bf16[768,768]{1,0:T(8,128)(2,1)} async-done(((bf16[48,768]{1,0:T(8,128)(2,1)}), bf16[768,768]{1,0:T(8,128)(2,1)}) %all-gather.22.cloned.1.call-update) | async-done | bytes 1179664 | tf_op jit(solution)/shard_map/all_gather | solution.py:110
  211.0 12.1 all-gather.1
  227.4 36.8 %while.56 = (s32[]{:T(128)}, bf16[12,1,256,64]{2,3,1,0:T(8,128)(2,1)}, f32[12,1,256,1]{2,3,1,0:T(1,128)}, bf16[12,1,256,64]{3,2,1,0:T(8,128)(2,1)}, bf16[12,1,51...) while((s32[]{:T(128)}, ...), condition=%wide.region_4.5_spmd.clone, body=%wide.region_1.4_spmd.clone.sunk | while | flops 35274496 | bytes 1949305 | solution.py:75
  267.4 20.6 %all-gather.26.cloned.1.call-done = bf16[768,768]{1,0:T(8,128)(2,1)} async-done(((bf16[48,768]{1,0:T(8,128)(2,1)}), bf16[768,768]{1,0:T(8,128)(2,1)}) %all-gather.26.cloned.1.call-update) | async-done | bytes 1179664 | tf_op jit(solution)/shard_map/all_gather | solution.py:118
  291.1 42.8 %all-gather.40.cloned.1.call-done = bf16[2048,768]{1,0:T(8,128)(2,1)} async-done(((bf16[1024,768]{1,0:T(8,128)(2,1)}), bf16[2048,768]{1,0:T(8,128)(2,1)}) %all-gather.40.cloned.1.call-update) | async-done | bytes 3145744 | tf_op jit(solution)/shard_map/all_gather | solution.py:200
  333.9 4.6 copy.77
  338.6 6.8 copy.80
  345.4 35.0 %all-gather.42.cloned.1.call-done = bf16[2048,768]{1,0:T(8,128)(2,1)} async-done(((bf16[1024,768]{1,0:T(8,128)(2,1)}), bf16[2048,768]{1,0:T(8,128)(2,1)}) %all-gather.42.cloned.1.call-update) | async-done | bytes 3145744 | tf_op jit(solution)/shard_map/all_gather | solution.py:201
  380.4 4.6 copy.78
  385.1 6.6 copy.81
  391.8 44.1 %while.54 = (s32[]{:T(128)}, bf16[12,1,256,64]{2,3,1,0:T(8,128)(2,1)S(1)}, f32[12,1,256,1]{2,3,1,0:T(1,128)S(1)}, bf16[12,1,256,64]{3,2,1,0:T(8,128)(2,1)}, bf16...) while((s32[]{:T(128)}, bf16[12,1,256,64]{2,3,1,0:T(8,128)(2,1)S(1)}, ...), condition=%wide.region_9.10_spmd, body=%wide.region_6.9_spmd.sunk | while | flops 137379584 | bytes 7449689 | solution.py:75
  438.9 28.6 %all-gather.34.cloned.1.call-done = bf16[768,2048]{1,0:T(8,128)(2,1)} async-done(((bf16[48,2048]{1,0:T(8,128)(2,1)}), bf16[768,2048]{1,0:T(8,128)(2,1)}) %all-gather.34.cloned.1.call-update) | async-done | bytes 3145744 | tf_op jit(solution)/shard_map/all_gather | solution.py:128
  467.5 4.2 fusion.157
  471.7 41.8 %all-gather.36.cloned.1.call-done = bf16[768,2048]{1,0:T(8,128)(2,1)} async-done(((bf16[48,2048]{1,0:T(8,128)(2,1)}), bf16[768,2048]{1,0:T(8,128)(2,1)}) %all-gather.36.cloned.1.call-update) | async-done | bytes 3145744 | tf_op jit(solution)/shard_map/all_gather | solution.py:129
  513.5 4.2 fusion.158
  517.7 41.9 %all-gather.38.cloned.1.call-done = bf16[2048,768]{1,0:T(8,128)(2,1)} async-done(((bf16[128,768]{1,0:T(8,128)(2,1)}), bf16[2048,768]{1,0:T(8,128)(2,1)}) %all-gather.38.cloned.1.call-update) | async-done | bytes 3145744 | tf_op jit(solution)/shard_map/all_gather | solution.py:130
  559.6 6.5 multiply_convert_fusion.2
  573.6 113.4 %while.55 = (s32[]{:T(128)}, bf16[12,1,256,64]{2,3,1,0:T(8,128)(2,1)S(1)}, bf16[12,1,2048,64]{2,3,1,0:T(8,128)(2,1)}, bf16[12,1,2048,64]{2,3,1,0:T(8,128)(2,1)},...) while((s32[]{:T(128)}, ...), condition=%wide.region_14.15_spmd, body=%wide.region_12.14_spmd.sunk | while | flops 339885824 | bytes 18622576 | solution.py:102
  694.4 93.0 %while.57 = (s32[]{:T(128)}, bf16[12,1,256,64]{2,3,1,0:T(8,128)(2,1)S(1)}, bf16[12,1,512,64]{2,3,1,0:T(8,128)(2,1)}, bf16[12,1,512,64]{2,3,1,0:T(8,128)(2,1)}, b...) while((s32[]{:T(128)}, ...), condition=%wide.region_18.19_spmd.clone, body=%wide.region_16.18_spmd.clone.sunk | while | flops 85901056 | bytes 4864657 | solution.py:102
  806.5 16.6 reduce-scatter.22.cloned.1.call-done
  826.2 3.7 fusion.161
  831.2 3.6 fusion.162
  836.1 3.7 fusion.133
  839.9 28.7 %reduce-scatter.24.cloned.1.call-done = bf16[1,1024,768]{1,2,0:T(8,128)(2,1)} async-done(((bf16[1,2048,768]{1,2,0:T(8,128)(2,1)}), bf16[1,1024,768]{1,2,0:T(8,128)(2,1)}) %reduce-scatter.24.cloned.1.call-update) | async-done | bytes 1572880 | tf_op jit(solution)/shard_map/reduce_scatter | solution.py:246
  868.6 4.2 convolution_bitcast_fusion.3
  876.2 38.0 %reduce-scatter.26.cloned.1.call-done = bf16[1,1024,768]{1,2,0:T(8,128)(2,1)} async-done(((bf16[1,2048,768]{1,2,0:T(8,128)(2,1)}), bf16[1,1024,768]{1,2,0:T(8,128)(2,1)}) %reduce-scatter.26.cloned.1.call-update) | async-done | bytes 1572880 | tf_op jit(solution)/shard_map/reduce_scatter | solution.py:249
  914.2 4.2 convolution_bitcast_fusion.2
  924.4 3.8 fusion.109
  931.0 50.1 %reduce-scatter.28.cloned.1.call-done = f32[48,768]{1,0:T(8,128)} async-done(((f32[768,768]{1,0:T(8,128)}), f32[48,768]{1,0:T(8,128)}) %reduce-scatter.28.cloned.1.call-update) | async-done | bytes 147472 | tf_op jit(solution)/shard_map/reduce_scatter | solution.py:317
  982.6 64.4 %reduce-scatter.34.cloned.1.call-done = f32[48,768]{1,0:T(8,128)} async-done(((f32[768,768]{1,0:T(8,128)}), f32[48,768]{1,0:T(8,128)}) %reduce-scatter.34.cloned.1.call-update) | async-done | bytes 147472 | tf_op jit(solution)/shard_map/reduce_scatter | solution.py:320
  1048.6 64.3 %reduce-scatter.36.cloned.1.call-done = f32[48,768]{1,0:T(8,128)} async-done(((f32[768,768]{1,0:T(8,128)}), f32[48,768]{1,0:T(8,128)}) %reduce-scatter.36.cloned.1.call-update) | async-done | bytes 147472 | tf_op jit(solution)/shard_map/reduce_scatter | solution.py:322
  1114.5 64.4 %reduce-scatter.38.cloned.1.call-done = f32[48,768]{1,0:T(8,128)} async-done(((f32[768,768]{1,0:T(8,128)}), f32[48,768]{1,0:T(8,128)}) %reduce-scatter.38.cloned.1.call-update) | async-done | bytes 147472 | tf_op jit(solution)/shard_map/reduce_scatter | solution.py:325
  1180.4 64.4 %reduce-scatter.30.cloned.1.call-done = f32[48,768]{1,0:T(8,128)} async-done(((f32[768,768]{1,0:T(8,128)}), f32[48,768]{1,0:T(8,128)}) %reduce-scatter.30.cloned.1.call-update) | async-done | bytes 147472 | tf_op jit(solution)/shard_map/reduce_scatter | solution.py:318
  1246.4 64.5 %reduce-scatter.32.cloned.1.call-done = f32[48,768]{1,0:T(8,128)} async-done(((f32[768,768]{1,0:T(8,128)}), f32[48,768]{1,0:T(8,128)}) %reduce-scatter.32.cloned.1.call-update) | async-done | bytes 147472 | tf_op jit(solution)/shard_map/reduce_scatter | solution.py:319
  1312.4 86.2 %reduce-scatter.40.cloned.1.call-done = f32[48,2048]{1,0:T(8,128)} async-done(((f32[768,2048]{1,0:T(8,128)}), f32[48,2048]{1,0:T(8,128)}) %reduce-scatter.40.cloned.1.call-update) | async-done | bytes 393232 | tf_op jit(solution)/shard_map/reduce_scatter | solution.py:327
  1400.4 86.5 %reduce-scatter.42.cloned.1.call-done = f32[48,2048]{1,0:T(8,128)} async-done(((f32[768,2048]{1,0:T(8,128)}), f32[48,2048]{1,0:T(8,128)}) %reduce-scatter.42.cloned.1.call-update) | async-done | bytes 393232 | tf_op jit(solution)/shard_map/reduce_scatter | solution.py:328
  1488.6 86.3 %reduce-scatter.44.cloned.1.call-done = f32[128,768]{1,0:T(8,128)} async-done(((f32[2048,768]{1,0:T(8,128)}), f32[128,768]{1,0:T(8,128)}) %reduce-scatter.44.cloned.1.call-update) | async-done | bytes 393232 | tf_op jit(solution)/shard_map/reduce_scatter | solution.py:329
  1576.5 64.6 %reduce-scatter.46.cloned.1.call-done = f32[48,768]{1,0:T(8,128)} async-done(((f32[768,768]{1,0:T(8,128)}), f32[48,768]{1,0:T(8,128)}) %reduce-scatter.46.cloned.1.call-update) | async-done | bytes 147472
  1642.8 64.5 %reduce-scatter.48.cloned.1.call-done = f32[48,768]{1,0:T(8,128)} async-done(((f32[768,768]{1,0:T(8,128)}), f32[48,768]{1,0:T(8,128)}) %reduce-scatter.48.cloned.1.call-update) | async-done | bytes 147472
  1710.3 57.6 %all-reduce.6 = (bf16[768]{0:T(1024)(128)(2,1)}, bf16[768]{0:T(1024)(128)(2,1)}, bf16[768]{0:T(1024)(128)(2,1)}) all-reduce(f32[768]{0:T(1024)} %get-tuple-element.390, f32[768]{0:T(1024)S(1)} %copy-done.41, f32[768]{0:T(1024)S(1)} %copy-done.40), channel_id=10, replica_groups=mesh['fsdp'=16,'seq'=2] {'fsdp'}, use_global_device_ids=true, to_apply=%region_25.26.clone | all-reduce | flops 2304 | bytes 13824
  1770.7 5.6 all-reduce.8
  (565 shorter events, 417.0 us)
Async XLA Ops:
  7.2 44.2 %copy-start = (bf16[1,1024,768]{2,1,0:T(8,128)(2,1)S(1)}, bf16[1,1024,768]{2,1,0:T(8,128)(2,1)}, u32[]{:S(2)}) copy-start(bf16[1,1024,768]{2,1,0:T(8,128)(2,1)} %param.28) | copy-start | bytes 4718596
  7.2 44.1 %all-gather.28.cloned.1.call-start = ((), (), s32[]{:S(2)}) async-start(), calls=%async_computation.20 | async-start | bytes 1253376 | tf_op jit(solution)/shard_map/all_gather | solution.py:119
  7.9 82.9 %all-gather.30.cloned.1.call-start = ((), (), s32[]{:S(2)}) async-start(), calls=%async_computation.21 | async-start | bytes 1253376 | tf_op jit(solution)/shard_map/all_gather | solution.py:120
  8.7 125.0 %all-gather.18.cloned.1.call-start = ((), (), s32[]{:S(2)}) async-start(), calls=%async_computation.15 | async-start | bytes 1253376 | tf_op jit(solution)/shard_map/all_gather | solution.py:108
  9.4 160.6 %all-gather.20.cloned.1.call-start = ((), (), s32[]{:S(2)}) async-start(), calls=%async_computation.16 | async-start | bytes 1253376 | tf_op jit(solution)/shard_map/all_gather | solution.py:109
  10.0 199.2 %all-gather.22.cloned.1.call-start = ((), (), s32[]{:S(2)}) async-start(), calls=%async_computation.17 | async-start | bytes 1253376 | tf_op jit(solution)/shard_map/all_gather | solution.py:110
  10.6 253.6 %all-gather.24.cloned.1.call-start = ((), (), s32[]{:S(2)}) async-start(), calls=%async_computation.18 | async-start | bytes 1253376 | tf_op jit(solution)/shard_map/all_gather | solution.py:111
  11.2 276.8 %all-gather.26.cloned.1.call-start = ((), (), s32[]{:S(2)}) async-start(), calls=%async_computation.19 | async-start | bytes 1253376 | tf_op jit(solution)/shard_map/all_gather | solution.py:118
  11.9 322.0 %all-gather.40.cloned.1.call-start = ((), (), s32[]{:S(2)}) async-start(), calls=%async_computation.39 | async-start | bytes 4718592 | tf_op jit(solution)/shard_map/all_gather | solution.py:200
  55.2 325.2 %all-gather.42.cloned.1.call-start = ((), (), s32[]{:S(2)}) async-start(), calls=%async_computation.40 | async-start | bytes 4718592 | tf_op jit(solution)/shard_map/all_gather | solution.py:201
  94.7 37.7 %copy-start.1 = (bf16[1,256,768]{2,1,0:T(8,128)(2,1)S(1)}, bf16[1,256,768]{2,1,0:T(8,128)(2,1)}, u32[]{:S(2)}) copy-start(bf16[1,256,768]{2,1,0:T(8,128)(2,1)} %param.27) | copy-start | bytes 1179652
  94.7 37.9 %copy-start.50 = (s32[1,512]{1,0:T(1,128)S(1)}, s32[1,512]{1,0:T(1,128)}, u32[]{:S(2)}) copy-start(s32[1,512]{1,0:T(1,128)} %param.30) | copy-start | bytes 6148
  94.7 38.4 %copy-start.51 = (s32[1,512]{1,0:T(1,128)S(1)}, s32[1,512]{1,0:T(1,128)}, u32[]{:S(2)}) copy-start(s32[1,512]{1,0:T(1,128)} %param.29) | copy-start | bytes 6148
  94.8 341.1 %all-gather.32.cloned.1.call-start = ((), (), s32[]{:S(2)}) async-start(), calls=%async_computation.22 | async-start | bytes 1253376 | tf_op jit(solution)/shard_map/all_gather | solution.py:121
  95.4 372.1 %all-gather.34.cloned.1.call-start = ((), (), s32[]{:S(2)}) async-start(), calls=%async_computation.23 | async-start | bytes 3342336 | tf_op jit(solution)/shard_map/all_gather | solution.py:128
  96.1 417.4 %all-gather.36.cloned.1.call-start = ((), (), s32[]{:S(2)}) async-start(), calls=%async_computation.24 | async-start | bytes 3342336 | tf_op jit(solution)/shard_map/all_gather | solution.py:129
  96.7 462.9 %all-gather.38.cloned.1.call-start = ((), (), s32[]{:S(2)}) async-start(), calls=%async_computation.25 | async-start | bytes 3342336 | tf_op jit(solution)/shard_map/all_gather | solution.py:130
  97.4 706.0 %reduce-scatter.20.cloned.1.call-start = ((), (), s32[]{:S(2)}) async-start(), calls=%async_computation.26 | async-start | bytes 1179648 | tf_op jit(solution)/shard_map/reduce_scatter | solution.py:279
  267.3 20.7 %copy-start.44 = (f32[256]{0:T(256)}, f32[256]{0:T(256)S(1)}, u32[]{:S(2)}) copy-start(f32[256]{0:T(256)S(1)} %get-tuple-element.501) | copy-start | bytes 3076
  267.4 20.7 %copy-start.37 = (f32[256]{0:T(256)}, f32[256]{0:T(256)S(1)}, u32[]{:S(2)}) copy-start(f32[256]{0:T(256)S(1)} %fusion.144) | copy-start | bytes 3076
  437.9 29.6 %copy-start.47 = (f32[256]{0:T(256)}, f32[256]{0:T(256)S(1)}, u32[]{:S(2)}) copy-start(f32[256]{0:T(256)S(1)} %get-tuple-element.503) | copy-start | bytes 3076
  437.9 29.6 %copy-start.42 = (f32[256]{0:T(256)}, f32[256]{0:T(256)S(1)}, u32[]{:S(2)}) copy-start(f32[256]{0:T(256)S(1)} %fusion.145) | copy-start | bytes 3076
  471.7 87.9 %copy-start.26 = (bf16[1,256,768]{2,1,0:T(8,128)(2,1)S(1)}, bf16[1,256,768]{2,1,0:T(8,128)(2,1)}, u32[]{:S(2)}) copy-start(bf16[1,256,768]{2,1,0:T(8,128)(2,1)} %param.31) | copy-start | bytes 1179652
  559.6 6.5 copy-start.23
  573.6 113.5 %copy-start.38 = (f32[256]{0:T(256)S(1)}, f32[256]{0:T(256)}, u32[]{:S(2)}) copy-start(f32[256]{0:T(256)} %copy-done.37) | copy-start | bytes 3076
  787.4 35.6 %reduce-scatter.22.cloned.1.call-start = ((), (), s32[]{:S(2)}) async-start(), calls=%async_computation.27 | async-start | bytes 1179648 | tf_op jit(solution)/shard_map/reduce_scatter | solution.py:282
  788.0 80.6 %reduce-scatter.24.cloned.1.call-start = ((), (), s32[]{:S(2)}) async-start(), calls=%async_computation.28 | async-start | bytes 4718592 | tf_op jit(solution)/shard_map/reduce_scatter | solution.py:246
  788.6 125.6 %reduce-scatter.26.cloned.1.call-start = ((), (), s32[]{:S(2)}) async-start(), calls=%async_computation.29 | async-start | bytes 4718592 | tf_op jit(solution)/shard_map/reduce_scatter | solution.py:249
  789.2 191.9 %reduce-scatter.28.cloned.1.call-start = ((), (), s32[]{:S(2)}) async-start(), calls=%async_computation.30 | async-start | bytes 2506752 | tf_op jit(solution)/shard_map/reduce_scatter | solution.py:317
  792.4 254.7 %reduce-scatter.34.cloned.1.call-start = ((), (), s32[]{:S(2)}) async-start(), calls=%async_computation.33 | async-start | bytes 2506752 | tf_op jit(solution)/shard_map/reduce_scatter | solution.py:320
  795.5 317.5 %reduce-scatter.36.cloned.1.call-start = ((), (), s32[]{:S(2)}) async-start(), calls=%async_computation.34 | async-start | bytes 2506752 | tf_op jit(solution)/shard_map/reduce_scatter | solution.py:322
  798.5 380.4 %reduce-scatter.38.cloned.1.call-start = ((), (), s32[]{:S(2)}) async-start(), calls=%async_computation.35 | async-start | bytes 2506752 | tf_op jit(solution)/shard_map/reduce_scatter | solution.py:325
  801.6 443.2 %reduce-scatter.30.cloned.1.call-start = ((), (), s32[]{:S(2)}) async-start(), calls=%async_computation.31 | async-start | bytes 2506752 | tf_op jit(solution)/shard_map/reduce_scatter | solution.py:318
  806.5 19.7 %copy-start.33 = (bf16[256,2048]{1,0:T(8,128)(2,1)S(1)}, bf16[256,2048]{1,0:T(8,128)(2,1)}, u32[]{:S(2)}) copy-start(bf16[256,2048]{1,0:T(8,128)(2,1)} %copy-done.32) | copy-start | bytes 3145732
  806.5 504.4 %reduce-scatter.32.cloned.1.call-start = ((), (), s32[]{:S(2)}) async-start(), calls=%async_computation.32 | async-start | bytes 2506752 | tf_op jit(solution)/shard_map/reduce_scatter | solution.py:319
  826.1 572.5 %reduce-scatter.40.cloned.1.call-start = ((), (), s32[]{:S(2)}) async-start(), calls=%async_computation.36 | async-start | bytes 6684672 | tf_op jit(solution)/shard_map/reduce_scatter | solution.py:327
  829.9 657.0 %reduce-scatter.42.cloned.1.call-start = ((), (), s32[]{:S(2)}) async-start(), calls=%async_computation.37 | async-start | bytes 6684672 | tf_op jit(solution)/shard_map/reduce_scatter | solution.py:328
  834.8 740.0 %reduce-scatter.44.cloned.1.call-start = ((), (), s32[]{:S(2)}) async-start(), calls=%async_computation.38 | async-start | bytes 6684672 | tf_op jit(solution)/shard_map/reduce_scatter | solution.py:329
  839.9 801.2 %reduce-scatter.46.cloned.1.call-start = ((), (), s32[]{:S(2)}) async-start(), calls=%async_computation.41 | async-start | bytes 2506752
  875.9 831.4 %reduce-scatter.48.cloned.1.call-start = ((), (), s32[]{:S(2)}) async-start(), calls=%async_computation.42 | async-start | bytes 2506752
  921.5 865.0 %all-reduce.12.cloned.1.call-start = ((), (), s32[]{:S(2)}) async-start(), calls=%async_computation.43 | async-start | bytes 2850816 | tf_op jit(solution)/shard_map/psum | solution.py:339
  1246.4 463.9 %copy-start.40 = (f32[768]{0:T(1024)S(1)}, f32[768]{0:T(1024)}, u32[]{:S(2)}) copy-start(f32[768]{0:T(1024)} %get-tuple-element.386) | copy-start | bytes 9220
  1246.4 463.9 %copy-start.41 = (f32[768]{0:T(1024)S(1)}, f32[768]{0:T(1024)}, u32[]{:S(2)}) copy-start(f32[768]{0:T(1024)} %get-tuple-element.388) | copy-start | bytes 9220
  1246.4 533.5 %copy-start.4 = (f32[256,768]{1,0:T(8,128)S(1)}, f32[256,768]{1,0:T(8,128)}, u32[]{:S(2)}) copy-start(f32[256,768]{1,0:T(8,128)} %copy-done.3) | copy-start | bytes 2359300
  1776.3 5.4 copy-start.54
  1786.6 12.8 copy-start.36
  1786.6 13.6 copy-start.35
  1786.6 14.4 copy-start.34
  (40 other events, 87.2 us)
Sparse Core Ops, SparseCore 0:
  10.3 41.0 all-gather.27
  53.6 37.1 all-gather.29
  93.1 37.4 all-gather.17
  132.7 37.2 all-gather.19
  172.1 37.0 all-gather.21
  211.3 37.0 all-gather.23
  250.7 37.2 all-gather.25
  290.1 43.7 all-gather.39
  335.5 44.8 all-gather.41
  382.6 38.2 all-gather.31
  423.2 44.3 all-gather.33
  469.6 43.7 all-gather.35
  515.7 43.7 all-gather.37
  787.6 15.8 reduce-scatter.19
  805.5 17.4 reduce-scatter.21
  825.2 43.3 reduce-scatter.23
  870.7 43.4 reduce-scatter.25
  917.8 63.2 reduce-scatter.27
  984.8 62.1 reduce-scatter.33
  1050.7 62.1 reduce-scatter.35
  1116.7 62.1 reduce-scatter.37
  1182.7 62.1 reduce-scatter.29
  1248.6 62.2 reduce-scatter.31
  1314.7 83.9 reduce-scatter.39
  1402.6 84.2 reduce-scatter.41
  1490.7 84.1 reduce-scatter.43
  1578.4 62.5 reduce-scatter.45
  1644.8 62.4 reduce-scatter.47
  1712.0 47.3 all-reduce.11
where the time goes:
time: 1820 us; the launch traced here: 1810 us
  waiting for transfers between devices  1200 us (66%)
  matrix products  339 us (19%)
  blocking collectives  120 us (7%)
  local copies, waits for them, and re-layouts  87.5 us (5%)
  other arithmetic  47.3 us (3%)
    unnamed x31, waiting for transfers between devices  138 us
    unnamed x2, blocking collectives  90 us
    reduce_scatter x1, waiting for transfers between devices, local(): lax.psum_scatter(all_grads[12], 'fsdp', scatter_dimension=0, tiled=True)  86.5 us
    reduce_scatter x1, waiting for transfers between devices, local(): lax.psum_scatter(all_grads[13], 'fsdp', scatter_dimension=0, tiled=True)  86.3 us
    reduce_scatter x1, waiting for transfers between devices, local(): lax.psum_scatter(all_grads[11], 'fsdp', scatter_dimension=0, tiled=True)  86.2 us
    dot_general x48, matrix products, score_block(): jnp.einsum('iqd,ikd->iqk', head_q, head_key_rows, preferred_element_type=...  73.9 us
    reduce_scatter x1, waiting for transfers between devices, local(): lax.psum_scatter(all_grads[3], 'fsdp', scatter_dimension=0, tiled=True)  64.5 us
    reduce_scatter x1, waiting for transfers between devices, local(): lax.psum_scatter(all_grads[9], 'fsdp', scatter_dimension=0, tiled=True)  64.4 us
  transfers between devices with their start and end apart: 29, of which 25 were waited for; matrix products, arithmetic and copies ran while one was open for 12% of the time, Pallas kernels for 0%

commit v1 on v0

v1 whole, which is shorter than its diff:
```python
import jax
import jax.numpy as jnp
from jax import lax
from jax.sharding import PartitionSpec as P

DH = 64
EPSILON = 1e-06
SCORE_SCALE = 0.125
MASKED = -1e30
BF = jnp.bfloat16
F4 = jnp.float32


def mm(a, b):
    return jnp.dot(a, b, preferred_element_type=F4)


def mm_nt(a, b):
    return lax.dot_general(a, b, (((1,), (1,)), ((), ())), preferred_element_type=F4)


def mm_tn(a, b):
    return lax.dot_general(a, b, (((0,), (0,)), ((), ())), preferred_element_type=F4)


def swap(value):
    return lax.ppermute(value, "seq", [(0, 1), (1, 0)])


def inv_rms(value):
    return lax.rsqrt(jnp.mean(value * value, axis=-1, keepdims=True) + EPSILON)


def norm_back(value, inv, gain, grad):
    unit = value * inv
    scaled = grad * gain
    dot = jnp.mean(scaled * unit, axis=-1, keepdims=True)
    return (scaled - unit * dot) * inv, jnp.sum(grad * unit, axis=0, keepdims=True)


def heads_of(value):
    return value.reshape(value.shape[0], -1, DH).transpose(1, 0, 2)


def rows_of(value):
    return value.transpose(1, 0, 2).reshape(value.shape[1], -1)


def attend_forward(query, key, value, allowed):
    def one_head(operands):
        q, k, v = operands
        scores = SCORE_SCALE * mm_nt(q, k)
        if allowed is not None:
            scores = jnp.where(allowed, scores, MASKED)
        highest = jnp.max(scores, axis=-1, keepdims=True)
        total = highest + jnp.log(jnp.sum(jnp.exp(scores - highest), axis=-1, keepdims=True))
        weights = jnp.exp(scores - total).astype(BF)
        return mm(weights, v).astype(BF), total

    mixed, totals = lax.map(one_head, (heads_of(query), heads_of(key), heads_of(value)))
    return rows_of(mixed), totals


def attend_backward(query, key, value, allowed, totals, grad):
    def one_head(operands):
        q, k, v, total, g = operands
        scores = SCORE_SCALE * mm_nt(q, k)
        if allowed is not None:
            scores = jnp.where(allowed, scores, MASKED)
        weights = jnp.exp(scores - total)
        dp = mm_nt(g, v)
        carried = jnp.sum(weights * dp, axis=-1, keepdims=True)
        ds = (weights * (dp - carried)).astype(BF)
        dq = (SCORE_SCALE * mm(ds, k)).astype(BF)
        dk = (SCORE_SCALE * mm_tn(ds, q)).astype(BF)
        dv = mm_tn(weights.astype(BF), g).astype(BF)
        return dq, dk, dv

    dq, dk, dv = lax.map(
        one_head, (heads_of(query), heads_of(key), heads_of(value), totals, heads_of(grad))
    )
    return rows_of(dq), rows_of(dk), rows_of(dv)


def gelu_parts(z):
    c = 0.7978845608028654
    t = jnp.tanh(c * (z + 0.044715 * z * z * z))
    act = 0.5 * z * (1.0 + t)
    slope = 0.5 * (1.0 + t) + 0.5 * z * (1.0 - t * t) * (c * (1.0 + 3.0 * 0.044715 * z * z))
    return act, slope


def local(
    tokens_in,
    patches,
    segment_ids,
    key_valid,
    out_grad,
    self_gain,
    self_query,
    self_key,
    self_value,
    self_output,
    cross_gain,
    cross_query,
    cross_key,
    cross_value,
    cross_output,
    mlp_gain,
    mlp_gate,
    mlp_up,
    mlp_down,
):
    side = lax.axis_index("seq")
    first = side == 0
    fsdp = lax.axis_size("fsdp")
    tok_half, width = tokens_in.shape[1:]
    patch_half = patches.shape[1]
    tok_total = segment_ids.shape[1]
    hidden = self_query.shape[1]
    half = hidden // 2
    ff_half = mlp_gate.shape[1] // 2
    ff_own = ff_half // fsdp
    own_row = side * tok_half
    own_col = side * half

    def ordered(mine, other, axis):
        return jnp.concatenate(
            [jnp.where(first, mine, other), jnp.where(first, other, mine)], axis=axis
        )

    def own_cols(weight):
        return lax.dynamic_slice_in_dim(weight, own_col, half, 1)

    def ff_cols(weight):
        split = weight.reshape(weight.shape[0], fsdp, 2, ff_own)
        mine = jnp.where(first, split[:, :, 0], split[:, :, 1])
        return mine.reshape(weight.shape[0], ff_half)

    gains = jnp.stack([self_gain, cross_gain, mlp_gain], axis=1)
    gains = jnp.pad(gains, ((0, 0), (0, 125)))
    cq_pair = jnp.concatenate(
        [
            jnp.where(first, cross_query[:, :half], cross_query[:, half:]),
            jnp.where(first, cross_query[:, half:], cross_query[:, :half]),
        ],
        axis=1,
    )
    shard = jnp.concatenate(
        [
            own_cols(self_query),
            own_cols(self_key),
            own_cols(self_value),
            gains,
            own_cols(cross_key),
            own_cols(cross_value),
            self_output,
            cq_pair,
            cross_output,
            ff_cols(mlp_gate),
            ff_cols(mlp_up),
        ],
        axis=1,
    )
    whole = lax.all_gather(shard, "fsdp", axis=0, tiled=True)
    w_down = lax.all_gather(
        lax.dynamic_slice_in_dim(mlp_down, side * ff_own, ff_own, 0), "fsdp", axis=0, tiled=True
    )
    at = 0
    pieces = []
    for size in (3 * half, 128, 2 * half, hidden, hidden, hidden, 2 * ff_half):
        pieces.append(whole[:, at : at + size])
        at += size
    w_qkv, gain_cols, w_ckv, w_so, w_cq, w_co, w_gu = pieces
    gain_rows = gain_cols.T.astype(F4)
    gain_one, gain_two, gain_three = gain_rows[0:1], gain_rows[1:2], gain_rows[2:3]

    tok_other = swap(tokens_in[0])
    grad_other = swap(out_grad[0])
    patch_other = swap(patches[0])
    x = ordered(tokens_in[0], tok_other, 0).astype(F4)
    g3 = ordered(out_grad[0], grad_other, 0)
    m = jnp.concatenate([patches[0], patch_other], axis=0)

    pos = jnp.arange(tok_total, dtype=jnp.int32)
    seg = segment_ids[0]
    valid = key_valid[0]
    allowed = (
        (seg[:, None] == seg[None, :])
        & (pos[None, :] <= pos[:, None])
        & ((valid[None, :] == 1) | (pos[None, :] == pos[:, None]))
    )

    inv_one = inv_rms(x)
    n1 = (x * inv_one * gain_one).astype(BF)
    qkv = mm(n1, w_qkv).astype(BF)
    q1, k1, v1 = qkv[:, :half], qkv[:, half : 2 * half], qkv[:, 2 * half :]
    o_own, lse_one = attend_forward(q1, k1, v1, allowed)
    o_all = ordered(o_own, swap(o_own), 1)
    h1 = x + mm(o_all, w_so)

    ckv = mm(m, w_ckv).astype(BF)
    kc, vc = ckv[:, :half], ckv[:, half:]
    inv_two = inv_rms(h1)
    n2 = (h1 * inv_two * gain_two).astype(BF)
    qc = mm(n2, w_cq[:, :half]).astype(BF)
    oc_own, lse_two = attend_forward(qc, kc, vc, None)
    oc_all = ordered(oc_own, swap(oc_own), 1)
    h2 = h1 + mm(oc_all, w_co)

    inv_three = inv_rms(h2)
    n3 = (h2 * inv_three * gain_three).astype(BF)
    ab = mm(n3, w_gu)
    act, slope = gelu_parts(ab[:, :ff_half])
    b = ab[:, ff_half:]
    u = (act * b).astype(BF)
    y = mm(u, w_down)

    def own_rows(value):
        return lax.dynamic_slice_in_dim(value, own_row, tok_half, 0)

    def other_rows(value):
        return lax.dynamic_slice_in_dim(value, tok_half - own_row, tok_half, 0)

    layer_out = (own_rows(h2) + own_rows(y) + swap(other_rows(y).astype(BF)).astype(F4)).astype(BF)

    du = mm_nt(g3, w_down)
    dab = jnp.concatenate([(du * b * slope).astype(BF), (du * act).astype(BF)], axis=1)
    dn3 = mm_nt(dab, w_gu)
    dn3 = dn3 + swap(dn3.astype(BF)).astype(F4)
    grad_gu = lax.psum_scatter(
        mm_tn(n3, dab).astype(BF), "fsdp", scatter_dimension=0, tiled=True
    )
    grad_down = lax.psum_scatter(mm_tn(u, g3).astype(BF), "fsdp", scatter_dimension=0, tiled=True)
    dh, gg3 = norm_back(h2, inv_three, gain_three, dn3)
    d1 = g3.astype(F4) + dh
    d1b = d1.astype(BF)

    grad_co = mm_tn(oc_all, own_cols(d1b)).astype(BF)
    doc = mm_nt(d1b, lax.dynamic_slice_in_dim(w_co, own_col, half, 0)).astype(BF)
    dqc, dkc, dvc = attend_backward(qc, kc, vc, None, lse_two, doc)
    dqc_pair = jnp.concatenate([dqc, swap(dqc)], axis=1)
    dh, gg2 = norm_back(h1, inv_two, gain_two, mm_nt(dqc_pair, w_cq))
    d2 = d1 + dh
    d2b = d2.astype(BF)
    dckv = jnp.concatenate([dkc, dvc], axis=1)
    part_other = mm_nt(dckv[patch_half:], w_ckv).astype(BF)
    patch_grad = mm_nt(dckv[:patch_half], w_ckv) + swap(part_other).astype(F4)
    grad_cq = mm_tn(n2, dqc).astype(BF)
    grad_ckv = mm_tn(m, dckv).astype(BF)

    grad_so = mm_tn(o_all, own_cols(d2b)).astype(BF)
    do = mm_nt(d2b, lax.dynamic_slice_in_dim(w_so, own_col, half, 0)).astype(BF)
    dqkv = jnp.concatenate(attend_backward(q1, k1, v1, allowed, lse_one, do), axis=1)
    grad_qkv = mm_tn(n1, dqkv).astype(BF)
    dn1 = mm_nt(dqkv, w_qkv)
    dn1 = own_rows(dn1) + swap(other_rows(dn1).astype(BF)).astype(F4)
    dx, gg1 = norm_back(own_rows(x), own_rows(inv_one), gain_one, dn1)
    input_grad = own_rows(d2) + dx

    gain_grads = jnp.concatenate([gg1, gg2, gg3, jnp.zeros((125, width), F4)], axis=0)
    packed = jnp.concatenate(
        [grad_co, grad_cq, grad_ckv, grad_so, grad_qkv, gain_grads.T.astype(BF)], axis=1
    )
    share = lax.psum_scatter(packed, "fsdp", scatter_dimension=0, tiled=True)

    share_other = swap(share)
    gu_other = swap(grad_gu)
    down_other = swap(grad_down)

    def pair(at):
        return ordered(share[:, at : at + half], share_other[:, at : at + half], 1).astype(F4)

    def ff_pair(at):
        mine = grad_gu[:, at : at + ff_half].reshape(-1, fsdp, 1, ff_own)
        other = gu_other[:, at : at + ff_half].reshape(-1, fsdp, 1, ff_own)
        return ordered(mine, other, 2).reshape(-1, 2 * ff_half).astype(F4)

    g_at = 8 * half
    mine = share[:, g_at : g_at + 3].astype(F4)
    other = share_other[:, g_at : g_at + 3].astype(F4)
    return (
        layer_out[None],
        input_grad[None],
        patch_grad[None],
        mine[:, 0] + other[:, 0],
        pair(5 * half),
        pair(6 * half),
        pair(7 * half),
        pair(4 * half),
        mine[:, 1],
        pair(half),
        pair(2 * half),
        pair(3 * half),
        pair(0),
        mine[:, 2],
        ff_pair(0),
        ff_pair(ff_half),
        ordered(grad_down, down_other, 0).astype(F4),
    )


def solution(mesh):
    rows = P("fsdp", None)
    items = P("fsdp", "seq", None)
    vec = P("fsdp")
    in_specs = (
        (items, items, rows, rows, items)
        + (vec, rows, rows, rows, rows) * 2
        + (vec, rows, rows, rows)
    )
    out_specs = (
        (items, items, items)
        + (vec, rows, rows, rows, rows) * 2
        + (vec, rows, rows, rows)
    )
    return jax.shard_map(local, mesh=mesh, in_specs=in_specs, out_specs=out_specs, check_vma=False)
```

time: 1820 us -> 491 us (0.27)
  waiting for transfers between devices: 1200 us -> 159 us
  matrix products: 339 us -> 209 us
  blocking collectives: 120 us -> 0 us
  local copies, waits for them, and re-layouts: 87.5 us -> 50.4 us
    reduce_scatter x13 -> x3, waiting for transfers between devices: 716 us -> 9.05 us  [the longest x1 9.05 us: local(): share = lax.psum_scatter(packed, 'fsdp', scatter_dimension=0, tiled=True)]
    all_gather x13 -> x2, waiting for transfers between devices: 343 us -> 63.5 us  [the longest x1 63.5 us: local(): whole = lax.all_gather(shard, 'fsdp', axis=0, tiled=True)]
    unnamed x31 -> x5, waiting for transfers between devices: 138 us -> 0.08 us
    dot_general x201 -> x106, matrix products: 339 us -> 209 us  [the longest x44 83.5 us: mm_nt(): lax.dot_general(a, b, (((1,), (1,)), ((), ())), preferred_element_type=F4)]
    unnamed x2 -> x0, blocking collectives: 90 us -> none
    ppermute x0 -> x13, waiting for transfers between devices: none -> 86 us  [swap(): return lax.ppermute(value, 'seq', [(0, 1), (1, 0)])]
    all_gather x2 -> x0, blocking collectives: 24 us -> none  [the longest x1 12.1 us: local(): lax.all_gather(value_one, 'seq', axis=1, tiled=True)]
    unnamed x137 -> x145, local copies, waits for them, and re-layouts: 33.6 us -> 12.2 us
  transfers between devices with their start and end apart: 29 -> 18, of which waited for: 25 -> 10; matrix products, arithmetic and copies ran while one was open for 12% -> 55% of each run, Pallas kernels for 0% -> 0%
where the time goes in v1:
time: 491 us; the launch traced here: 486 us
  matrix products  209 us (43%)
  waiting for transfers between devices  159 us (32%)
  local copies, waits for them, and re-layouts  50.4 us (10%)
  other arithmetic  34.7 us (7%)
  starting transfers between devices  16.8 us (3%)
  between operations  15.1 us (3%)
    ppermute x13, waiting for transfers between devices, swap(): return lax.ppermute(value, 'seq', [(0, 1), (1, 0)])  86 us
    dot_general x44, matrix products, mm_nt(): lax.dot_general(a, b, (((1,), (1,)), ((), ())), preferred_element_type=F4)  83.5 us
    all_gather x1, waiting for transfers between devices, local(): whole = lax.all_gather(shard, 'fsdp', axis=0, tiled=True)  63.5 us
    dot_general x31, matrix products, mm_tn(): lax.dot_general(a, b, (((0,), (0,)), ((), ())), preferred_element_type=F4)  63.1 us
    dot_general x31, matrix products, mm(): return jnp.dot(a, b, preferred_element_type=F4)  62.4 us
    ppermute x13, starting transfers between devices, swap(): return lax.ppermute(value, 'seq', [(0, 1), (1, 0)])  16.1 us
    reshape x5, local copies, waits for them, and re-layouts, heads_of(): return value.reshape(value.shape[0], -1, DH).transpose(1, 0, 2)  12.9 us
    unnamed x145, local copies, waits for them, and re-layouts  12.2 us
  transfers between devices with their start and end apart: 18, of which 10 were waited for; matrix products, arithmetic and copies ran while one was open for 55% of the time, Pallas kernels for 0%

profile of v1, /device:TPU:0, one launch (start us, length us, event | category | flops | bytes accessed | tf_op | source)
XLA Modules:
  0.0 485.5 jit_solution(5060921676663346116)
XLA Ops:
  14.0 3.0 collective-permute-start.5
  20.3 6.7 %collective-permute-done.5 = bf16[256,768]{1,0:T(8,128)(2,1)S(1)} collective-permute-done((bf16[256,768]{1,0:T(8,128)(2,1)S(1)}, bf16[256,768]{1,0:T(8,128)(2,1)S(1)}, u32[]{:S(2)}, u32[]{:S(2)}) %collective-permute-start.5) | collective-permute-done | bytes 393248 | tf_op jit(solution)/shard_map/ppermute | solution.py:27
  27.0 8.4 %collective-permute-done = bf16[256,768]{1,0:T(8,128)(2,1)S(1)} collective-permute-done((bf16[256,768]{1,0:T(8,128)(2,1)S(1)}, bf16[256,768]{1,0:T(8,128)(2,1)S(1)}, u32[]{:S(2)}, u32[]{:S(2)}) %collective-permute-start) | collective-permute-done | bytes 393248 | tf_op jit(solution)/shard_map/ppermute | solution.py:27
  36.7 63.5 %all-gather.3.cloned.1.call-done = bf16[768,6400]{1,0:T(8,128)(2,1)} async-done(((bf16[48,6400]{1,0:T(8,128)(2,1)}), bf16[768,6400]{1,0:T(8,128)(2,1)}) %all-gather.3.cloned.1.call-update) | async-done | bytes 9830416 | tf_op jit(solution)/shard_map/all_gather | solution.py:165
  101.8 2.7 convolution_convert_fusion.6
  107.2 9.3 %while.56 = (s32[]{:T(128)}, bf16[6,512,64]{1,2,0:T(8,128)(2,1)}, f32[6,512,1]{1,2,0:T(1,128)S(1)}, bf16[6,512,64]{2,1,0:T(8,128)(2,1)S(1)}, bf16[6,512,64]{2,1,...) while((s32[]{:T(128)}, bf16[6,512,64]{1,2,0:T(8,128)(2,1)}, ...), condition=%wide.region_4.5_spmd.clone, body=%wide.region_1.4_spmd.clone.sunk | while | flops 70548992 | bytes 3629673 | solution.py:60
  118.0 4.9 %convolution_convert_fusion.5 = bf16[2048,768]{0,1:T(8,128)(2,1)S(1)} fusion(bf16[1024,768]{1,0:T(8,128)(2,1)} %collective-permute-done.2, bf16[1024,768]{1,0:T(8,128)(2,1)} %bitcast.300, bf16[768,6400]{1,0:T(8,128)(2,1)} %all-gather.3.cloned.1.call-done), kind=kOutput, calls=%fused_computation.132 | convolution fusion | flops 2423783424 | bytes 7471104 | tf_op jit(solution)/shard_map/dot_general | solution.py:15
  124.8 3.2 copy.63
  127.9 4.1 copy.64
  133.4 2.4 multiply_reduce_fusion.8
  137.1 2.4 convolution_convert_fusion.14
  142.5 31.3 %while.54 = (s32[]{:T(128)}, bf16[6,512,64]{1,2,0:T(8,128)(2,1)}, f32[6,512,1]{1,2,0:T(1,128)S(1)}, bf16[6,512,64]{2,1,0:T(8,128)(2,1)}, bf16[6,2048,64]{2,1,0:T...) while((s32[]{:T(128)}, bf16[6,512,64]{1,2,0:T(8,128)(2,1)}, f32[6,512,1]{1,2,0:T(1,128)S(1)}, ...), condition=%wide.region_9.10_spmd, body=%wide.region_6.9_spmd.sunk | while | flops 276856320 | bytes 13848665 | solution.py:60
  145.0 2.7 fusion.212
  150.2 2.7 fusion.212
  155.4 2.7 fusion.212
  160.6 2.7 fusion.212
  165.8 2.7 fusion.212
  171.0 2.7 fusion.212
  174.5 10.4 %collective-permute-done.3 = bf16[512,384]{0,1:T(8,128)(2,1)S(1)} collective-permute-done((bf16[512,384]{0,1:T(8,128)(2,1)}, bf16[512,384]{0,1:T(8,128)(2,1)S(1)}, u32[]{:S(2)}, u32[]{:S(2)}) %collective-permute-start.3) | collective-permute-done | bytes 393248 | tf_op jit(solution)/shard_map/ppermute | solution.py:27
  186.1 2.5 multiply_reduce_fusion.7
  189.7 5.8 %fusion.101 = f32[512,2048]{1,0:T(8,128)} fusion(bf16[768,6400]{1,0:T(8,128)(2,1)} %all-gather.3.cloned.1.call-done, f32[512,768]{1,0:T(8,128)S(1)} %get-tuple-element.405, f32[768]{0:T(1024)S(1)} %get-tuple-element.272, f32[512]{0:T(512)S(1)} %add_rsqrt_fusion), kind=kOutput, calls=%fused_computation.141 | convolution fusion | flops 1611792384 | bytes 8918016 | tf_op jit(solution)/shard_map/dot_general | solution.py:15
  195.5 6.6 %fusion.110 = (bf16[512,1024]{1,0:T(8,128)(2,1)}, bf16[512,1024]{1,0:T(8,128)(2,1)}, bf16[512,1024]{1,0:T(8,128)(2,1)S(1)}) fusion(f32[512,2048]{1,0:T(8,128)} %fusion.101, bf16[1024,768]{1,0:T(8,128)(2,1)} %all-gather.5.cloned.1.call-done, bf16[256,768]{1,0:T(8,128)(2,1)} %get-tuple-element.369, bf16[256,768]{1,0:T(8,128)(2,1)} %get-tuple-element.368), kind=kOutput, calls=%fused_computation.150 | convolution fusion | flops 819986432 | bytes 9699328 | tf_op jit(solution)/shard_map/dot_general | solution.py:19
  203.1 2.2 convolution_convert_fusion.7
  205.6 5.9 %fusion.169 = (bf16[512,768]{1,0:T(8,128)(2,1)}, f32[512,768]{1,0:T(8,128)}) fusion(bf16[768,6400]{1,0:T(8,128)(2,1)} %all-gather.3.cloned.1.call-done, bf16[512,1024]{1,0:T(8,128)(2,1)} %get-tuple-element.361, bf16[512,1024]{1,0:T(8,128)(2,1)} %get-tuple-element.360), kind=kOutput, calls=%fused_computation.322 | convolution fusion | flops 1615200256 | bytes 7602176 | tf_op jit(solution)/shard_map/dot_general | solution.py:19
  213.8 3.4 fusion.164
  217.2 3.6 convolution_convert_fusion.3
  220.9 9.4 %collective-permute-done.6 = bf16[512,768]{1,0:T(8,128)(2,1)} collective-permute-done((bf16[512,768]{1,0:T(8,128)(2,1)}, bf16[512,768]{1,0:T(8,128)(2,1)}, u32[]{:S(2)}, u32[]{:S(2)}) %collective-permute-start.6) | collective-permute-done | bytes 786464 | tf_op jit(solution)/shard_map/ppermute | solution.py:27
  230.3 2.8 multiply_reduce_fusion.3
  233.5 2.9 fusion.162
  242.0 61.2 %while.55 = (s32[]{:T(128)}, bf16[6,512,64]{1,2,0:T(8,128)(2,1)}, bf16[6,2048,64]{1,2,0:T(8,128)(2,1)}, bf16[6,2048,64]{1,2,0:T(8,128)(2,1)}, bf16[6,512,64]{2,1...) while((s32[]{:T(128)}, bf16[6,512,64]{1,2,0:T(8,128)(2,1)}, ...), condition=%wide.region_14.15_spmd, body=%wide.region_12.14_spmd.sunk | while | flops 679935488 | bytes 34159728 | solution.py:79
  244.1 2.2 multiply_reduce_fusion.16
  254.2 2.2 multiply_reduce_fusion.16
  264.4 2.2 multiply_reduce_fusion.16
  274.5 2.2 multiply_reduce_fusion.16
  284.7 2.2 multiply_reduce_fusion.16
  307.3 6.5 %fusion.121 = bf16[768,768]{0,1:T(8,128)(2,1)} fusion(bf16[1024,768]{1,0:T(8,128)(2,1)} %collective-permute-done.2, bf16[1024,768]{1,0:T(8,128)(2,1)} %bitcast.301, bf16[2048,384]{0,1:T(8,128)(2,1)} %bitcast.302, bf16[2048,384]{0,1:T(8,128)(2,1)} %bitcast.305), kind=kOutput, calls=%fused_computation.176 | convolution fusion | flops 2429091840 | bytes 7471104 | tf_op jit(solution)/shard_map/dot_general | solution.py:23
  318.8 2.7 multiply_reduce_fusion.4
  327.7 45.1 %while.57 = (s32[]{:T(128)}, bf16[6,512,64]{1,2,0:T(8,128)(2,1)}, bf16[6,512,64]{1,2,0:T(8,128)(2,1)}, bf16[6,512,64]{1,2,0:T(8,128)(2,1)}, bf16[6,512,64]{2,1,0...) while((s32[]{:T(128)}, bf16[6,512,64]{1,2,0:T(8,128)(2,1)}, ...), condition=%wide.region_18.19_spmd.clone, body=%wide.region_16.18_spmd.clone.sunk | while | flops 171867648 | bytes 8998529 | solution.py:79
  372.9 2.5 convolution_convert_fusion.10
  376.7 3.1 fusion.118
  382.1 2.7 fusion.97
  384.8 4.6 collective-permute-done.8
  391.2 4.6 convolution_convert_fusion.8
  399.0 39.2 %collective-permute-done.4 = bf16[256,768]{1,0:T(8,128)(2,1)S(1)} collective-permute-done((bf16[256,768]{1,0:T(8,128)(2,1)S(1)}, bf16[256,768]{1,0:T(8,128)(2,1)S(1)}, u32[]{:S(2)}, u32[]{:S(2)}) %collective-permute-start.4) | collective-permute-done | bytes 393248 | tf_op jit(solution)/shard_map/ppermute | solution.py:27
  440.6 5.4 %add_bitcast_fusion = f32[1,1024,768]{2,1,0:T(8,128)} fusion(bf16[1024,768]{1,0:T(8,128)(2,1)} %collective-permute-done.9, bf16[2048,384]{0,1:T(8,128)(2,1)} %bitcast.307, bf16[2048,384]{0,1:T(8,128)(2,1)} %bitcast.304, bf16[768,6400]{1,0:T(8,128)(2,1)} %all-gather.3.cloned.1.call-done), kind=kOutput, calls=%fused_computation.135 | convolution fusion | flops 1212678144 | bytes 9043968 | tf_op jit(solution)/shard_map/dot_general | solution.py:19
  448.5 3.3 collective-permute-done.11
  455.7 9.0 %reduce-scatter.4.cloned.1.call-done = bf16[48,3200]{1,0:T(8,128)(2,1)} async-done(((bf16[768,3200]{1,0:T(8,128)(2,1)}), bf16[48,3200]{1,0:T(8,128)(2,1)}) %reduce-scatter.4.cloned.1.call-update) | async-done | bytes 307216 | tf_op jit(solution)/shard_map/reduce_scatter | solution.py:265
  468.4 3.9 collective-permute-done.10
  (399 shorter events, 198.3 us)
Async XLA Ops:
  7.2 11.9 %copy-start = (bf16[128,768]{1,0:T(8,128)(2,1)S(1)}, bf16[128,768]{1,0:T(8,128)(2,1)}, u32[]{:S(2)}) copy-start(bf16[128,768]{1,0:T(8,128)(2,1)} %param.45) | copy-start | bytes 589828
  7.2 93.0 %all-gather.3.cloned.1.call-start = ((), (), s32[]{:S(2)}) async-start(), calls=%async_computation.3 | async-start | bytes 10444800 | tf_op jit(solution)/shard_map/all_gather | solution.py:165
  12.1 5.0 %copy-start.46 = (bf16[1,256,768]{2,1,0:T(8,128)(2,1)S(1)}, bf16[1,256,768]{2,1,0:T(8,128)(2,1)}, u32[]{:S(2)}) copy-start(bf16[1,256,768]{2,1,0:T(8,128)(2,1)} %param.27) | copy-start | bytes 1179652
  12.1 8.2 %copy-start.57 = (s32[1,512]{1,0:T(1,128)S(1)}, s32[1,512]{1,0:T(1,128)}, u32[]{:S(2)}) copy-start(s32[1,512]{1,0:T(1,128)} %param.30) | copy-start | bytes 6148
  13.9 181.6 %all-gather.5.cloned.1.call-start = ((), (), s32[]{:S(2)}) async-start(), calls=%async_computation.4 | async-start | bytes 1671168 | tf_op jit(solution)/shard_map/all_gather | solution.py:166
  14.0 13.0 %collective-permute-start.5 = (bf16[256,768]{1,0:T(8,128)(2,1)S(1)}, bf16[256,768]{1,0:T(8,128)(2,1)S(1)}, u32[]{:S(2)}, u32[]{:S(2)}) collective-permute-start(bf16[256,768]{1,0:T(8,128)(2,1)S(1)} %bitcast.292), channel_id=1, source_target_pairs={{0,1},{1,0},{2,3},{3,2},{4,5},{5,4},{6,7},{7,6},{8,9},{9,8},{10,11... | collective-permute-start | bytes 1179656 | tf_op jit(solution)/shard_map/ppermute | solution.py:27
  17.0 18.4 %collective-permute-start = (bf16[256,768]{1,0:T(8,128)(2,1)S(1)}, bf16[256,768]{1,0:T(8,128)(2,1)S(1)}, u32[]{:S(2)}, u32[]{:S(2)}) collective-permute-start(bf16[256,768]{1,0:T(8,128)(2,1)S(1)} %bitcast.293), channel_id=1, source_target_pairs={{0,1},{1,0},{2,3},{3,2},{4,5},{5,4},{6,7},{7,6},{8,9},{9,8},{10,11... | collective-permute-start | bytes 1179656 | tf_op jit(solution)/shard_map/ppermute | solution.py:27
  17.1 100.9 %collective-permute-start.2 = (bf16[1024,768]{1,0:T(8,128)(2,1)}, bf16[1024,768]{1,0:T(8,128)(2,1)}, u32[]{:S(2)}, u32[]{:S(2)}) collective-permute-start(bf16[1024,768]{1,0:T(8,128)(2,1)} %bitcast.299), channel_id=1, source_target_pairs={{0,1},{1,0},{2,3},{3,2},{4,5},{5,4},{6,7},{7,6},{8,9},{9,8},{10,11... | collective-permute-start | bytes 4718600 | tf_op jit(solution)/shard_map/ppermute | solution.py:27
  19.7 420.5 %reduce-scatter.8.cloned.1.call-start = ((), (), s32[]{:S(2)}) async-start(), calls=%async_computation.7 | async-start | bytes 1671168 | tf_op jit(solution)/shard_map/reduce_scatter | solution.py:234
  36.4 68.1 %copy-start.13 = (bf16[256,768]{1,0:T(8,128)(2,1)}, bf16[256,768]{1,0:T(8,128)(2,1)S(1)}, u32[]{:S(2)}) copy-start(bf16[256,768]{1,0:T(8,128)(2,1)S(1)} %get-tuple-element.409) | copy-start | bytes 1179652
  36.4 68.1 %copy-start.17 = (bf16[256,768]{1,0:T(8,128)(2,1)}, bf16[256,768]{1,0:T(8,128)(2,1)S(1)}, u32[]{:S(2)}) copy-start(bf16[256,768]{1,0:T(8,128)(2,1)S(1)} %get-tuple-element.410) | copy-start | bytes 1179652
  116.5 6.4 %copy-start.12 = (bf16[6,512,64]{2,1,0:T(8,128)(2,1)}, bf16[6,512,64]{2,1,0:T(8,128)(2,1)S(1)}, u32[]{:S(2)}) copy-start(bf16[6,512,64]{2,1,0:T(8,128)(2,1)S(1)} %get-tuple-element.759) | copy-start | bytes 1179652
  116.5 6.4 %copy-start.21 = (bf16[6,512,64]{2,1,0:T(8,128)(2,1)}, bf16[6,512,64]{2,1,0:T(8,128)(2,1)S(1)}, u32[]{:S(2)}) copy-start(bf16[6,512,64]{2,1,0:T(8,128)(2,1)S(1)} %get-tuple-element.762) | copy-start | bytes 1179652
  116.5 6.4 %copy-start.22 = (bf16[6,512,64]{2,1,0:T(8,128)(2,1)}, bf16[6,512,64]{2,1,0:T(8,128)(2,1)S(1)}, u32[]{:S(2)}) copy-start(bf16[6,512,64]{2,1,0:T(8,128)(2,1)S(1)} %get-tuple-element.763) | copy-start | bytes 1179652
  116.5 15.6 %collective-permute-start.1 = (bf16[512,384]{0,1:T(8,128)(2,1)}, bf16[512,384]{0,1:T(8,128)(2,1)}, u32[]{:S(2)}, u32[]{:S(2)}) collective-permute-start(bf16[512,384]{0,1:T(8,128)(2,1)} %bitcast.26), channel_id=1, source_target_pairs={{0,1},{1,0},{2,3},{3,2},{4,5},{5,4},{6,7},{7,6},{8,9},{9,8},{10,11... | collective-permute-start | bytes 1179656 | tf_op jit(solution)/shard_map/ppermute | solution.py:27
  173.8 12.2 %copy-start.3 = (f32[512,768]{1,0:T(8,128)S(1)}, f32[512,768]{1,0:T(8,128)}, u32[]{:S(2)}) copy-start(f32[512,768]{1,0:T(8,128)} %copy-done.2) | copy-start | bytes 4718596
  173.8 11.2 %collective-permute-start.3 = (bf16[512,384]{0,1:T(8,128)(2,1)}, bf16[512,384]{0,1:T(8,128)(2,1)S(1)}, u32[]{:S(2)}, u32[]{:S(2)}) collective-permute-start(bf16[512,384]{0,1:T(8,128)(2,1)} %bitcast.274), channel_id=1, source_target_pairs={{0,1},{1,0},{2,3},{3,2},{4,5},{5,4},{6,7},{7,6},{8,9},{9,8},{10,11... | collective-permute-start | bytes 1179656 | tf_op jit(solution)/shard_map/ppermute | solution.py:27
  195.5 7.5 %copy-start.28 = (bf16[256,768]{1,0:T(8,128)(2,1)S(1)}, bf16[256,768]{1,0:T(8,128)(2,1)}, u32[]{:S(2)}) copy-start(bf16[256,768]{1,0:T(8,128)(2,1)} %get-tuple-element.368) | copy-start | bytes 1179652
  195.5 7.5 %copy-start.30 = (bf16[256,768]{1,0:T(8,128)(2,1)S(1)}, bf16[256,768]{1,0:T(8,128)(2,1)}, u32[]{:S(2)}) copy-start(bf16[256,768]{1,0:T(8,128)(2,1)} %get-tuple-element.369) | copy-start | bytes 1179652
  205.3 240.6 %reduce-scatter.6.cloned.1.call-start = ((), (), s32[]{:S(2)}) async-start(), calls=%async_computation.6 | async-start | bytes 3342336 | tf_op jit(solution)/shard_map/reduce_scatter | solution.py:231
  205.5 7.0 %copy-start.15 = (bf16[256,768]{1,0:T(8,128)(2,1)S(1)}, bf16[256,768]{1,0:T(8,128)(2,1)}, u32[]{:S(2)}) copy-start(bf16[256,768]{1,0:T(8,128)(2,1)} %copy-done.13) | copy-start | bytes 1179652
  205.6 7.0 %copy-start.19 = (bf16[256,768]{1,0:T(8,128)(2,1)S(1)}, bf16[256,768]{1,0:T(8,128)(2,1)}, u32[]{:S(2)}) copy-start(bf16[256,768]{1,0:T(8,128)(2,1)} %copy-done.17) | copy-start | bytes 1179652
  211.5 18.8 %collective-permute-start.6 = (bf16[512,768]{1,0:T(8,128)(2,1)}, bf16[512,768]{1,0:T(8,128)(2,1)}, u32[]{:S(2)}, u32[]{:S(2)}) collective-permute-start(bf16[512,768]{1,0:T(8,128)(2,1)} %get-tuple-element.406), channel_id=1, source_target_pairs={{0,1},{1,0},{2,3},{3,2},{4,5},{5,4},{6,7},{7,6},{8,9},{9,8},{10,11... | collective-permute-start | bytes 2359304 | tf_op jit(solution)/shard_map/ppermute | solution.py:27
  213.8 3.4 copy-start.6
  213.8 3.4 copy-start.62
  213.8 3.4 copy-start.63
  220.8 243.9 %reduce-scatter.4.cloned.1.call-start = ((), (), s32[]{:S(2)}) async-start(), calls=%async_computation.5 | async-start | bytes 5222400 | tf_op jit(solution)/shard_map/reduce_scatter | solution.py:265
  230.3 3.1 copy-start.10
  230.3 3.2 copy-start.29
  230.3 3.3 copy-start.31
  233.5 2.9 copy-start.44
  303.3 3.6 copy-start.35
  303.3 15.5 %collective-permute-start.7 = (bf16[512,384]{0,1:T(8,128)(2,1)}, bf16[512,384]{0,1:T(8,128)(2,1)}, u32[]{:S(2)}, u32[]{:S(2)}) collective-permute-start(bf16[512,384]{0,1:T(8,128)(2,1)} %bitcast.278), channel_id=1, source_target_pairs={{0,1},{1,0},{2,3},{3,2},{4,5},{5,4},{6,7},{7,6},{8,9},{9,8},{10,11... | collective-permute-start | bytes 1179656 | tf_op jit(solution)/shard_map/ppermute | solution.py:27
  379.8 9.5 %copy-start.23 = (f32[512,768]{1,0:T(8,128)}, f32[512,768]{1,0:T(8,128)S(1)}, u32[]{:S(2)}) copy-start(f32[512,768]{1,0:T(8,128)S(1)} %fusion.118) | copy-start | bytes 4718596
  379.9 9.4 %collective-permute-start.8 = (bf16[256,768]{1,0:T(8,128)(2,1)S(1)}, bf16[256,768]{1,0:T(8,128)(2,1)S(1)}, u32[]{:S(2)}, u32[]{:S(2)}) collective-permute-start(bf16[256,768]{1,0:T(8,128)(2,1)S(1)} %dynamic-slice_convert_fusion), channel_id=1, source_target_pairs={{0,1},{1,0},{2,3},{3,2},{4,5},{5,4},{6,7},{7,6},{8,9},{9,8},{10,11... | collective-permute-start | bytes 1179656 | tf_op jit(solution)/shard_map/ppermute | solution.py:27
  382.1 7.3 %copy-start.9 = (f32[512,768]{1,0:T(8,128)S(1)}, f32[512,768]{1,0:T(8,128)}, u32[]{:S(2)}) copy-start(f32[512,768]{1,0:T(8,128)} %fusion.160) | copy-start | bytes 4718596
  391.2 5.0 %copy-start.58 = (bf16[1024,768]{1,0:T(8,128)(2,1)S(1)}, bf16[1024,768]{1,0:T(8,128)(2,1)}, u32[]{:S(2)}) copy-start(bf16[1024,768]{1,0:T(8,128)(2,1)} %all-gather.5.cloned.1.call-done) | copy-start | bytes 4718596
  391.2 5.0 %copy-start.61 = (bf16[512,1024]{1,0:T(8,128)(2,1)S(1)}, bf16[512,1024]{1,0:T(8,128)(2,1)}, u32[]{:S(2)}) copy-start(bf16[512,1024]{1,0:T(8,128)(2,1)} %copy-done.60) | copy-start | bytes 3145732
  395.8 42.4 %copy-start.8 = (f32[512,768]{1,0:T(8,128)S(1)}, f32[512,768]{1,0:T(8,128)}, u32[]{:S(2)}) copy-start(f32[512,768]{1,0:T(8,128)} %copy-done.5) | copy-start | bytes 4718596
  395.8 44.7 %collective-permute-start.9 = (bf16[1024,768]{1,0:T(8,128)(2,1)}, bf16[1024,768]{1,0:T(8,128)(2,1)}, u32[]{:S(2)}, u32[]{:S(2)}) collective-permute-start(bf16[1024,768]{1,0:T(8,128)(2,1)} %convolution_convert_fusion.8), channel_id=1, source_target_pairs={{0,1},{1,0},{2,3},{3,2},{4,5},{5,4},{6,7},{7,6},{8,9},{9,8},{10,11... | collective-permute-start | bytes 4718600 | tf_op jit(solution)/shard_map/ppermute | solution.py:27
  397.2 41.9 %copy-start.24 = (f32[512,768]{1,0:T(8,128)S(1)}, f32[512,768]{1,0:T(8,128)}, u32[]{:S(2)}) copy-start(f32[512,768]{1,0:T(8,128)} %copy-done.23) | copy-start | bytes 4718596
  397.2 41.9 %copy-start.27 = (bf16[256,768]{1,0:T(8,128)(2,1)S(1)}, bf16[256,768]{1,0:T(8,128)(2,1)}, u32[]{:S(2)}) copy-start(bf16[256,768]{1,0:T(8,128)(2,1)} %copy-done.26) | copy-start | bytes 1179652
  397.3 40.9 %collective-permute-start.4 = (bf16[256,768]{1,0:T(8,128)(2,1)S(1)}, bf16[256,768]{1,0:T(8,128)(2,1)S(1)}, u32[]{:S(2)}, u32[]{:S(2)}) collective-permute-start(bf16[256,768]{1,0:T(8,128)(2,1)S(1)} %dynamic-slice_convert_fusion.1), channel_id=1, source_target_pairs={{0,1},{1,0},{2,3},{3,2},{4,5},{5,4},{6,7},{7,6},{8,9},{9,8},{10,11... | collective-permute-start | bytes 1179656 | tf_op jit(solution)/shard_map/ppermute | solution.py:27
  440.3 7.4 %copy-start.49 = (bf16[64,768]{1,0:T(8,128)(2,1)S(1)}, bf16[64,768]{1,0:T(8,128)(2,1)}, u32[]{:S(2)}) copy-start(bf16[64,768]{1,0:T(8,128)(2,1)} %reduce-scatter.8.cloned.1.call-done) | copy-start | bytes 294916
  440.3 7.4 %collective-permute-start.12 = (bf16[64,768]{1,0:T(8,128)(2,1)}, bf16[64,768]{1,0:T(8,128)(2,1)S(1)}, u32[]{:S(2)}, u32[]{:S(2)}) collective-permute-start(bf16[64,768]{1,0:T(8,128)(2,1)} %reduce-scatter.8.cloned.1.call-done), channel_id=1, source_target_pairs={{0,1},{1,0},{2,3},{3,2},{4,5},{5,4},{6,7},{7,6},{8,9},{9,8},{10,11... | collective-permute-start | bytes 294920 | tf_op jit(solution)/shard_map/ppermute | solution.py:27
  446.0 5.9 %collective-permute-start.11 = (bf16[48,2048]{1,0:T(8,128)(2,1)}, bf16[48,2048]{1,0:T(8,128)(2,1)S(1)}, u32[]{:S(2)}, u32[]{:S(2)}) collective-permute-start(bf16[48,2048]{1,0:T(8,128)(2,1)} %reduce-scatter.6.cloned.1.call-done), channel_id=1, source_target_pairs={{0,1},{1,0},{2,3},{3,2},{4,5},{5,4},{6,7},{7,6},{8,9},{9,8},{10,11... | collective-permute-start | bytes 589832 | tf_op jit(solution)/shard_map/ppermute | solution.py:27
  464.8 7.6 %collective-permute-start.10 = (bf16[48,3200]{1,0:T(8,128)(2,1)}, bf16[48,3200]{1,0:T(8,128)(2,1)S(1)}, u32[]{:S(2)}, u32[]{:S(2)}) collective-permute-start(bf16[48,3200]{1,0:T(8,128)(2,1)} %reduce-scatter.4.cloned.1.call-done), channel_id=1, source_target_pairs={{0,1},{1,0},{2,3},{3,2},{4,5},{5,4},{6,7},{7,6},{8,9},{9,8},{10,11... | collective-permute-start | bytes 921608 | tf_op jit(solution)/shard_map/ppermute | solution.py:27
  468.4 10.1 %copy-start.1 = (bf16[128,768]{1,0:T(8,128)(2,1)S(1)}, bf16[128,768]{1,0:T(8,128)(2,1)}, u32[]{:S(2)}) copy-start(bf16[128,768]{1,0:T(8,128)(2,1)} %param.45) | copy-start | bytes 589828
  (34 other events, 56.8 us)
Sparse Core Ops, SparseCore 0:
  14.1 86.0 all-gather.2
  103.1 37.9 all-gather.4
  205.4 57.4 reduce-scatter.7
  266.6 65.3 reduce-scatter.5
  391.3 73.3 reduce-scatter.3

commit v2 on v1

--- a/solution.py
+++ b/solution.py
@@ -1,6 +1,10 @@
+import functools
+
 import jax
 import jax.numpy as jnp
 from jax import lax
+from jax.experimental import pallas as pl
+from jax.experimental.pallas import tpu as pltpu
 from jax.sharding import PartitionSpec as P
 
 DH = 64
@@ -38,48 +42,150 @@
     return (scaled - unit * dot) * inv, jnp.sum(grad * unit, axis=0, keepdims=True)
 
 
-def heads_of(value):
-    return value.reshape(value.shape[0], -1, DH).transpose(1, 0, 2)
-
-
-def rows_of(value):
-    return value.transpose(1, 0, 2).reshape(value.shape[1], -1)
-
-
-def attend_forward(query, key, value, allowed):
-    def one_head(operands):
-        q, k, v = operands
-        scores = SCORE_SCALE * mm_nt(q, k)
-        if allowed is not None:
-            scores = jnp.where(allowed, scores, MASKED)
-        highest = jnp.max(scores, axis=-1, keepdims=True)
-        total = highest + jnp.log(jnp.sum(jnp.exp(scores - highest), axis=-1, keepdims=True))
-        weights = jnp.exp(scores - total).astype(BF)
-        return mm(weights, v).astype(BF), total
-
-    mixed, totals = lax.map(one_head, (heads_of(query), heads_of(key), heads_of(value)))
-    return rows_of(mixed), totals
-
-
-def attend_backward(query, key, value, allowed, totals, grad):
-    def one_head(operands):
-        q, k, v, total, g = operands
-        scores = SCORE_SCALE * mm_nt(q, k)
-        if allowed is not None:
-            scores = jnp.where(allowed, scores, MASKED)
-        weights = jnp.exp(scores - total)
-        dp = mm_nt(g, v)
-        carried = jnp.sum(weights * dp, axis=-1, keepdims=True)
-        ds = (weights * (dp - carried)).astype(BF)
-        dq = (SCORE_SCALE * mm(ds, k)).astype(BF)
-        dk = (SCORE_SCALE * mm_tn(ds, q)).astype(BF)
-        dv = mm_tn(weights.astype(BF), g).astype(BF)
-        return dq, dk, dv
-
-    dq, dk, dv = lax.map(
-        one_head, (heads_of(query), heads_of(key), heads_of(value), totals, heads_of(grad))
-    )
-    return rows_of(dq), rows_of(dk), rows_of(dv)
+def lanes_of_head():
+    odd = lax.rem(pl.program_id(0), 2)
+    lane = lax.broadcasted_iota(jnp.int32, (1, 2 * DH), 1)
+    return odd, (lane >= DH) == (odd == 1)
+
+
+def keep_lanes(ref, at, value, odd, mine):
+    value = value.astype(ref.dtype)
+
+    @pl.when(odd == 0)
+    def _():
+        ref[at] = value
+
+    @pl.when(odd == 1)
+    def _():
+        ref[at] = jnp.where(mine, value, ref[at])
+
+
+def fold_rows(value):
+    return value.reshape(value.shape[0] // 8, 8, value.shape[1])
+
+
+def forward_kernel(masked, chunk, q_ref, k_ref, v_ref, *rest):
+    bias_ref = rest[0] if masked else None
+    o_ref, inv_ref, e_ref, s_ref, acc_ref = rest[-5:]
+    odd, mine = lanes_of_head()
+    count = k_ref.shape[0] // chunk
+    q = jnp.where(mine, q_ref[...].astype(F4) * SCORE_SCALE, 0.0).astype(BF)
+    top = jnp.full((8, q.shape[0]), -jnp.inf, F4)
+    for c in range(count):
+        rows = pl.ds(c * chunk, chunk)
+        scores = mm_nt(k_ref[rows, :], q)
+        if masked:
+            scores = scores + bias_ref[rows, :]
+        s_ref[rows, :] = scores
+        top = jnp.maximum(top, jnp.max(fold_rows(scores), axis=0))
+    top = jnp.max(top, axis=0, keepdims=True)
+    total = jnp.zeros((8, q.shape[0]), F4)
+    for c in range(count):
+        rows = pl.ds(c * chunk, chunk)
+        e = jnp.exp(s_ref[rows, :] - top)
+        total = total + jnp.sum(fold_rows(e), axis=0)
+        e = e.astype(BF)
+        e_ref[0, rows, :] = e
+        part = mm_tn(v_ref[rows, :], e)
+        acc_ref[...] = part if c == 0 else acc_ref[...] + part
+    inv = 1.0 / jnp.sum(total, axis=0, keepdims=True)
+    whole = (slice(None), slice(None))
+    keep_lanes(o_ref, whole, (acc_ref[...] * inv).T, odd, mine)
+    keep_lanes(inv_ref, whole, jnp.broadcast_to(inv, acc_ref.shape).T, odd, mine)
+
+
+def attend_forward(query, key, value, bias):
+    rows, width = query.shape
+    keys = key.shape[0]
+    heads = width // DH
+    chunk = min(keys, 512)
+
+    def pair(size):
+        return pl.BlockSpec((size, 2 * DH), lambda h: (0, h // 2))
+
+    specs = [pair(rows), pair(keys), pair(keys)]
+    args = [query, key, value]
+    if bias is not None:
+        specs.append(pl.BlockSpec((keys, rows), lambda h: (0, 0)))
+        args.append(bias)
+    return pl.pallas_call(
+        functools.partial(forward_kernel, bias is not None, chunk),
+        grid=(heads,),
+        in_specs=specs,
+        out_specs=[pair(rows), pair(rows), pl.BlockSpec((1, keys, rows), lambda h: (h, 0, 0))],
+        out_shape=[
+            jax.ShapeDtypeStruct((rows, width), BF),
+            jax.ShapeDtypeStruct((rows, width), F4),
+            jax.ShapeDtypeStruct((heads, keys, rows), BF),
+        ],
+        scratch_shapes=[pltpu.VMEM((keys, rows), F4), pltpu.VMEM((2 * DH, rows), F4)],
+        compiler_params=pltpu.CompilerParams(vmem_limit_bytes=40 << 20),
+        cost_estimate=pl.CostEstimate(
+            flops=4 * heads * rows * keys * 256,
+            bytes_accessed=2 * heads * rows * keys,
+            transcendentals=heads * rows * keys,
+        ),
+        name="attend_forward",
+    )(*args)
+
+
+def backward_kernel(chunk, e_ref, q_ref, k_ref, v_ref, g_ref, o_ref, dq_ref, dk_ref, dv_ref, acc_ref):
+    odd, mine = lanes_of_head()
+    count = k_ref.shape[0] // chunk
+    q = (q_ref[...].astype(F4) * SCORE_SCALE).astype(BF)
+    g = g_ref[...]
+    own = jnp.where(mine, g.astype(F4), 0.0)
+    carried = jnp.sum((own * o_ref[...].astype(F4)).T, axis=0, keepdims=True)
+    own = own.astype(BF)
+    for c in range(count):
+        rows = pl.ds(c * chunk, chunk)
+        e = e_ref[0, rows, :]
+        dp = mm_nt(v_ref[rows, :], own)
+        ds = (e.astype(F4) * (dp - carried)).astype(BF)
+        at = (rows, slice(None))
+        keep_lanes(dv_ref, at, mm(e, g), odd, mine)
+        keep_lanes(dk_ref, at, mm(ds, q), odd, mine)
+        part = mm_tn(k_ref[rows, :], ds)
+        acc_ref[...] = part if c == 0 else acc_ref[...] + part
+    keep_lanes(dq_ref, (slice(None), slice(None)), acc_ref[...].T * SCORE_SCALE, odd, mine)
+
+
+def attend_backward(query, key, value, mixed, inv, weights, grad):
+    rows, width = query.shape
+    keys = key.shape[0]
+    heads = width // DH
+    chunk = min(keys, 512)
+    grad = (grad.astype(F4) * inv).astype(BF)
+
+    def pair(size):
+        return pl.BlockSpec((size, 2 * DH), lambda h: (0, h // 2))
+
+    return pl.pallas_call(
+        functools.partial(backward_kernel, chunk),
+        grid=(heads,),
+        in_specs=[
+            pl.BlockSpec((1, keys, rows), lambda h: (h, 0, 0)),
+            pair(rows),
+            pair(keys),
+            pair(keys),
+            pair(rows),
+            pair(rows),
+        ],
+        out_specs=[pair(rows), pair(keys), pair(keys)],
+        out_shape=[
+            jax.ShapeDtypeStruct((rows, width), BF),
+            jax.ShapeDtypeStruct((keys, width), BF),
+            jax.ShapeDtypeStruct((keys, width), BF),
+        ],
+        scratch_shapes=[pltpu.VMEM((2 * DH, rows), F4)],
+        compiler_params=pltpu.CompilerParams(vmem_limit_bytes=40 << 20),
+        cost_estimate=pl.CostEstimate(
+            flops=8 * heads * rows * keys * 256,
+            bytes_accessed=2 * heads * rows * keys,
+            transcendentals=0,
+        ),
+        name="attend_backward",
+    )(weights, query, key, value, grad, mixed)
 
 
 def gelu_parts(z):
@@ -187,15 +293,16 @@
     valid = key_valid[0]
     allowed = (
         (seg[:, None] == seg[None, :])
-        & (pos[None, :] <= pos[:, None])
-        & ((valid[None, :] == 1) | (pos[None, :] == pos[:, None]))
-    )
+        & (pos[:, None] <= pos[None, :])
+        & ((valid[:, None] == 1) | (pos[:, None] == pos[None, :]))
+    )
+    bias = jnp.where(allowed, 0.0, MASKED).astype(F4)
 
     inv_one = inv_rms(x)
     n1 = (x * inv_one * gain_one).astype(BF)
     qkv = mm(n1, w_qkv).astype(BF)
     q1, k1, v1 = qkv[:, :half], qkv[:, half : 2 * half], qkv[:, 2 * half :]
-    o_own, lse_one = attend_forward(q1, k1, v1, allowed)
+    o_own, inv_l1, e1 = attend_forward(q1, k1, v1, bias)
     o_all = ordered(o_own, swap(o_own), 1)
     h1 = x + mm(o_all, w_so)
 
@@ -204,7 +311,7 @@
     inv_two = inv_rms(h1)
     n2 = (h1 * inv_two * gain_two).astype(BF)
     qc = mm(n2, w_cq[:, :half]).astype(BF)
-    oc_own, lse_two = attend_forward(qc, kc, vc, None)
+    oc_own, inv_l2, e2 = attend_forward(qc, kc, vc, None)
     oc_all = ordered(oc_own, swap(oc_own), 1)
     h2 = h1 + mm(oc_all, w_co)
 
@@ -238,7 +345,7 @@
 
     grad_co = mm_tn(oc_all, own_cols(d1b)).astype(BF)
     doc = mm_nt(d1b, lax.dynamic_slice_in_dim(w_co, own_col, half, 0)).astype(BF)
-    dqc, dkc, dvc = attend_backward(qc, kc, vc, None, lse_two, doc)
+    dqc, dkc, dvc = attend_backward(qc, kc, vc, oc_own, inv_l2, e2, doc)
     dqc_pair = jnp.concatenate([dqc, swap(dqc)], axis=1)
     dh, gg2 = norm_back(h1, inv_two, gain_two, mm_nt(dqc_pair, w_cq))
     d2 = d1 + dh
@@ -251,7 +358,7 @@
 
     grad_so = mm_tn(o_all, own_cols(d2b)).astype(BF)
     do = mm_nt(d2b, lax.dynamic_slice_in_dim(w_so, own_col, half, 0)).astype(BF)
-    dqkv = jnp.concatenate(attend_backward(q1, k1, v1, allowed, lse_one, do), axis=1)
+    dqkv = jnp.concatenate(attend_backward(q1, k1, v1, o_own, inv_l1, e1, do), axis=1)
     grad_qkv = mm_tn(n1, dqkv).astype(BF)
     dn1 = mm_nt(dqkv, w_qkv)
     dn1 = own_rows(dn1) + swap(other_rows(dn1).astype(BF)).astype(F4)

time: 491 us -> 404 us (0.82)
  matrix products: 209 us -> 62.9 us
  Pallas kernels: 0 us -> 62.8 us
  waiting for transfers between devices: 159 us -> 170 us
  other arithmetic: 34.7 us -> 25.2 us
  local copies, waits for them, and re-layouts: 50.4 us -> 45.1 us
    pallas_call x0 -> x4, Pallas kernels: none -> 62.8 us  [the longest x2 41.1 us: attend_backward(): pl.pallas_call(functools.partial(backward_kernel, chunk), grid=(heads,),...]
    dot_general x44 -> x8, matrix products: 83.5 us -> 29.8 us  [mm_nt(): lax.dot_general(a, b, (((1,), (1,)), ((), ())), preferred_element_type=F4)]
    dot_general x31 -> x7, matrix products: 62.4 us -> 14.1 us  [mm(): return jnp.dot(a, b, preferred_element_type=F4)]
    dot_general x31 -> x7, matrix products: 63.1 us -> 19 us  [mm_tn(): lax.dot_general(a, b, (((0,), (0,)), ((), ())), preferred_element_type=F4)]
    reshape x5 -> x0, local copies, waits for them, and re-layouts: 12.9 us -> none  [heads_of(): return value.reshape(value.shape[0], -1, DH).transpose(1, 0, 2)]
    reduce_scatter x1, waiting for transfers between devices: 9.05 us -> 20.1 us  [local(): share = lax.psum_scatter(packed, 'fsdp', scatter_dimension=0, tiled=True)]
    unnamed x145 -> x179, local copies, waits for them, and re-layouts: 12.2 us -> 21.8 us
    reduce_sum x12 -> x0, other arithmetic: 6.14 us -> none  [one_head(): jnp.sum(jnp.exp(scores - highest), axis=-1, keepdims=True)]
  transfers between devices with their start and end apart: 18 -> 18, of which waited for: 10 -> 11; matrix products, arithmetic and copies ran while one was open for 55% -> 24% of each run, Pallas kernels for 0% -> 16%
where the time goes in v2:
time: 404 us; the launch traced here: 399 us
  waiting for transfers between devices  170 us (42%)
  matrix products  62.9 us (16%)
  Pallas kernels  62.8 us (16%)
  local copies, waits for them, and re-layouts  45.1 us (11%)
  other arithmetic  25.2 us (6%)
  starting transfers between devices  17.4 us (4%)
  between operations  14.9 us (4%)
    ppermute x13, waiting for transfers between devices, swap(): return lax.ppermute(value, 'seq', [(0, 1), (1, 0)])  87.7 us
    all_gather x1, waiting for transfers between devices, local(): whole = lax.all_gather(shard, 'fsdp', axis=0, tiled=True)  62.4 us
    pallas_call x2, Pallas kernels, attend_backward(): pl.pallas_call(functools.partial(backward_kernel, chunk), grid=(heads,),...  41.1 us
    dot_general x8, matrix products, mm_nt(): lax.dot_general(a, b, (((1,), (1,)), ((), ())), preferred_element_type=F4)  29.8 us
    unnamed x179, local copies, waits for them, and re-layouts  21.8 us
    pallas_call x2, Pallas kernels, attend_forward(): pl.pallas_call(functools.partial(forward_kernel, bias is not None, chunk)...  21.7 us
    reduce_scatter x1, waiting for transfers between devices, local(): share = lax.psum_scatter(packed, 'fsdp', scatter_dimension=0, tiled=True)  20.1 us
    dot_general x7, matrix products, mm_tn(): lax.dot_general(a, b, (((0,), (0,)), ((), ())), preferred_element_type=F4)  19 us
  transfers between devices with their start and end apart: 18, of which 11 were waited for; matrix products, arithmetic and copies ran while one was open for 24% of the time, Pallas kernels for 16%

profile of v2, /device:TPU:0, one launch (start us, length us, event | category | flops | bytes accessed | tf_op | source)
XLA Modules:
  0.0 398.5 jit_solution(4176999176610716934)
XLA Ops:
  19.2 3.0 collective-permute-start
  22.3 1.9 collective-permute-start.2
  25.3 6.9 %collective-permute-done = bf16[256,768]{1,0:T(8,128)(2,1)S(1)} collective-permute-done((bf16[256,768]{1,0:T(8,128)(2,1)S(1)}, bf16[256,768]{1,0:T(8,128)(2,1)S(1)}, u32[]{:S(2)}, u32[]{:S(2)}) %collective-permute-start) | collective-permute-done | bytes 393248 | tf_op jit(solution)/shard_map/ppermute | solution.py:31
  32.2 8.5 %collective-permute-done.5 = bf16[256,768]{1,0:T(8,128)(2,1)} collective-permute-done((bf16[256,768]{1,0:T(8,128)(2,1)S(1)}, bf16[256,768]{1,0:T(8,128)(2,1)}, u32[]{:S(2)}, u32[]{:S(2)}) %collective-permute-start.5) | collective-permute-done | bytes 393248 | tf_op jit(solution)/shard_map/ppermute | solution.py:31
  40.7 2.0 broadcast_select_fusion.5
  43.0 62.4 %all-gather.3.cloned.1.call-done = bf16[768,6400]{1,0:T(8,128)(2,1)} async-done(((bf16[48,6400]{1,0:T(8,128)(2,1)}), bf16[768,6400]{1,0:T(8,128)(2,1)}) %all-gather.3.cloned.1.call-update) | async-done | bytes 9830416 | tf_op jit(solution)/shard_map/all_gather | solution.py:271
  107.0 2.9 convolution_convert_fusion.3
  110.0 6.3 %attend_forward.2 = (bf16[512,384]{1,0:T(8,128)(2,1)S(1)}, f32[512,384]{1,0:T(8,128)S(1)}, bf16[6,512,512]{2,1,0:T(8,128)(2,1)S(1)}) custom-call(bf16[512,384]{1,0:T(8,128)(2,1)S(1)} %get-tuple-element.66.q_ref, bf16[512,384]{1,0:T(8,128)(2,1)S(1)} %get-tuple-element.65.k_ref, bf16[512,384]{1,0:T(8,128)(2,1)S(1)} %get-tuple-element.64.v_ref, ...), custom_call_target="tpu_custom_call" | custom-call | flops 1610612736 | bytes 3145728 | tf_op jit(solution)/shard_map/attend_forward/pallas_call | solution.py:111
  117.2 1.7 copy-done.18
  118.9 1.5 collective-permute-start.1
  120.4 4.0 %convolution_convert_fusion.2 = bf16[2048,768]{1,0:T(8,128)(2,1)S(1)} fusion(bf16[1024,768]{1,0:T(8,128)(2,1)} %collective-permute-done.2, bf16[1024,768]{1,0:T(8,128)(2,1)S(1)} %bitcast.48, bf16[768,6400]{1,0:T(8,128)(2,1)S(1)} %copy-done.46), kind=kOutput, calls=%fused_computation.3 | convolution fusion | flops 2423783424 | bytes 7471104 | tf_op jit(solution)/shard_map/dot_general | solution.py:19
  124.8 5.4 %collective-permute-done.1 = bf16[512,384]{1,0:T(8,128)(2,1)S(1)} collective-permute-done((bf16[512,384]{1,0:T(8,128)(2,1)S(1)}, bf16[512,384]{1,0:T(8,128)(2,1)S(1)}, u32[]{:S(2)}, u32[]{:S(2)}) %collective-permute-start.1) | collective-permute-done | bytes 393248 | tf_op jit(solution)/shard_map/ppermute | solution.py:31
  131.8 15.4 %attend_forward.3 = (bf16[512,384]{1,0:T(8,128)(2,1)S(1)}, f32[512,384]{1,0:T(8,128)S(1)}, bf16[6,2048,512]{2,1,0:T(8,128)(2,1)}) custom-call(bf16[512,384]{1,0:T(8,128)(2,1)S(1)} %convolution_convert_fusion.11.q_ref, bf16[2048,384]{1,0:T(8,128)(2,1)S(1)} %get-tuple-element.63.k_ref, bf16[2048,384]{1,0:T(8,128)(2,1)S(1)} %get-tuple-element.62.v_ref), custom_call_target="tpu_custom_call" | custom-call | flops 6442450944 | bytes 12582912 | tf_op jit(solution)/shard_map/attend_forward/pallas_call | solution.py:111
  147.2 1.5 collective-permute-start.3
  148.7 9.0 %collective-permute-done.3 = bf16[512,384]{1,0:T(8,128)(2,1)S(1)} collective-permute-done((bf16[512,384]{1,0:T(8,128)(2,1)S(1)}, bf16[512,384]{1,0:T(8,128)(2,1)S(1)}, u32[]{:S(2)}, u32[]{:S(2)}) %collective-permute-start.3) | collective-permute-done | bytes 393248 | tf_op jit(solution)/shard_map/ppermute | solution.py:31
  159.8 3.8 fusion.3
  163.7 5.7 %fusion.12 = (bf16[512,1024]{1,0:T(8,128)(2,1)}, bf16[512,1024]{1,0:T(8,128)(2,1)}, bf16[512,1024]{1,0:T(8,128)(2,1)S(1)}) fusion(f32[512,2048]{1,0:T(8,128)} %fusion.3, bf16[1024,768]{1,0:T(8,128)(2,1)} %all-gather.5.cloned.1.call-done, bf16[256,768]{1,0:T(8,128)(2,1)S(1)} %copy-done.44, bf16[256,768]{1,0:T(8,128)(2,1)S(1)} %copy-done.42), kind=kOutput, calls=%fused_computation.20 | convolution fusion | flops 819986432 | bytes 9699328 | tf_op jit(solution)/shard_map/dot_general | solution.py:23
  170.3 2.2 convolution_convert_fusion.4
  174.2 5.5 %fusion.75 = (bf16[512,768]{1,0:T(8,128)(2,1)}, f32[512,768]{1,0:T(8,128)}) fusion(bf16[768,6400]{1,0:T(8,128)(2,1)} %all-gather.3.cloned.1.call-done, bf16[512,1024]{1,0:T(8,128)(2,1)} %get-tuple-element.60, bf16[512,1024]{1,0:T(8,128)(2,1)S(1)} %copy-done.78), kind=kOutput, calls=%fused_computation.204 | convolution fusion | flops 1615200256 | bytes 7602176 | tf_op jit(solution)/shard_map/dot_general | solution.py:23
  182.5 3.4 fusion.70
  186.0 3.6 convolution_convert_fusion
  189.7 8.3 %collective-permute-done.6 = bf16[512,768]{1,0:T(8,128)(2,1)} collective-permute-done((bf16[512,768]{1,0:T(8,128)(2,1)}, bf16[512,768]{1,0:T(8,128)(2,1)}, u32[]{:S(2)}, u32[]{:S(2)}) %collective-permute-start.6) | collective-permute-done | bytes 786464 | tf_op jit(solution)/shard_map/ppermute | solution.py:31
  198.0 2.9 multiply_reduce_fusion
  201.0 3.0 fusion.69
  205.9 31.8 %attend_backward.2 = (bf16[512,384]{1,0:T(8,128)(2,1)}, bf16[2048,384]{1,0:T(8,128)(2,1)S(1)}, bf16[2048,384]{1,0:T(8,128)(2,1)S(1)}) custom-call(bf16[6,2048,512]{2,1,0:T(8,128)(2,1)} %get-tuple-element.31.e_ref, bf16[512,384]{1,0:T(8,128)(2,1)S(1)} %copy-done.17, bf16[2048,384]{1,0:T(8,128)(2,1)S(1)} %copy-done.5, bf16[2048,384]{1,0:T(8,128)(2,1)S(1)} %copy-done.3, ...), custom_call_target="tpu_custom_call" | custom-call | flops 12884901888 | bytes 12582912 | tf_op jit(solution)/shard_map/attend_backward/pallas_call | solution.py:163
  237.7 1.5 collective-permute-start.7
  239.1 2.4 convolution_convert_fusion.7
  241.6 2.2 copy.52
  248.6 6.3 %fusion.22 = bf16[768,768]{0,1:T(8,128)(2,1)} fusion(bf16[2048,768]{1,0:T(8,128)(2,1)} %constant_dynamic-update-slice_fusion.15, bf16[1024,768]{1,0:T(8,128)(2,1)} %collective-permute-done.2, bf16[1024,768]{1,0:T(8,128)(2,1)S(1)} %bitcast.49), kind=kOutput, calls=%fused_computation.47 | convolution fusion | flops 2422800384 | bytes 7471104 | tf_op jit(solution)/shard_map/dot_general | solution.py:27
  254.9 1.6 copy.53
  260.4 3.6 multiply_reduce_fusion.1
  266.5 2.1 copy.54
  268.6 1.8 fusion.25.g_ref
  270.4 1.9 copy-done.19
  272.3 9.3 %attend_backward.3 = (bf16[512,384]{1,0:T(8,128)(2,1)S(1)}, bf16[512,384]{1,0:T(8,128)(2,1)S(1)}, bf16[512,384]{1,0:T(8,128)(2,1)S(1)}) custom-call(bf16[6,512,512]{2,1,0:T(8,128)(2,1)S(1)} %copy-done.19, bf16[512,384]{1,0:T(8,128)(2,1)S(1)} %copy-done.11, bf16[512,384]{1,0:T(8,128)(2,1)S(1)} %copy-done.9, bf16[512,384]{1,0:T(8,128)(2,1)S(1)} %get-tuple-element.64.v_ref, ...), custom_call_target="tpu_custom_call" | custom-call | flops 3221225472 | bytes 3145728 | tf_op jit(solution)/shard_map/attend_backward/pallas_call | solution.py:163
  281.9 2.8 fusion.19
  286.4 2.7 fusion
  289.1 3.9 collective-permute-done.8
  294.5 4.6 %convolution_convert_fusion.5 = bf16[1024,768]{1,0:T(8,128)(2,1)} fusion(bf16[2048,768]{1,0:T(8,128)(2,1)} %constant_dynamic-update-slice_fusion.15, bf16[768,6400]{1,0:T(8,128)(2,1)} %all-gather.3.cloned.1.call-done), kind=kOutput, calls=%fused_computation.27 | convolution fusion | flops 1208745984 | bytes 4325376 | tf_op jit(solution)/shard_map/dot_general | solution.py:23
  300.5 1.7 collective-permute-start.4
  302.2 38.2 %collective-permute-done.4 = bf16[256,768]{1,0:T(8,128)(2,1)S(1)} collective-permute-done((bf16[256,768]{1,0:T(8,128)(2,1)S(1)}, bf16[256,768]{1,0:T(8,128)(2,1)S(1)}, u32[]{:S(2)}, u32[]{:S(2)}) %collective-permute-start.4) | collective-permute-done | bytes 393248 | tf_op jit(solution)/shard_map/ppermute | solution.py:31
  343.0 5.3 %add_bitcast_fusion = f32[1,1024,768]{2,1,0:T(8,128)} fusion(bf16[1024,768]{1,0:T(8,128)(2,1)} %collective-permute-done.9, bf16[2048,768]{1,0:T(8,128)(2,1)} %constant_dynamic-update-slice_fusion.15, bf16[768,6400]{1,0:T(8,128)(2,1)} %all-gather.3.cloned.1.call-done), kind=kOutput, calls=%fused_computation.5 | convolution fusion | flops 1209532416 | bytes 7471104 | tf_op jit(solution)/shard_map/dot_general | solution.py:23
  348.3 1.5 collective-permute-start.11
  350.6 3.6 collective-permute-done.11
  356.2 1.4 reshape.213
  358.0 20.1 %reduce-scatter.4.cloned.1.call-done = bf16[48,3200]{1,0:T(8,128)(2,1)} async-done(((bf16[768,3200]{1,0:T(8,128)(2,1)}), bf16[48,3200]{1,0:T(8,128)(2,1)}) %reduce-scatter.4.cloned.1.call-update) | async-done | bytes 307216 | tf_op jit(solution)/shard_map/reduce_scatter | solution.py:372
  378.1 1.5 collective-permute-start.10
  381.8 3.8 collective-permute-done.10
  (274 shorter events, 57.3 us)
Async XLA Ops:
  7.2 17.1 %copy-start = (bf16[128,768]{1,0:T(8,128)(2,1)S(1)}, bf16[128,768]{1,0:T(8,128)(2,1)}, u32[]{:S(2)}) copy-start(bf16[128,768]{1,0:T(8,128)(2,1)} %param.37) | copy-start | bytes 589828
  7.2 9.2 %copy-start.60 = (bf16[48,2048]{1,0:T(8,128)(2,1)S(1)}, bf16[48,2048]{1,0:T(8,128)(2,1)}, u32[]{:S(2)}) copy-start(bf16[48,2048]{1,0:T(8,128)(2,1)} %param.35) | copy-start | bytes 589828
  7.2 98.2 %all-gather.3.cloned.1.call-start = ((), (), s32[]{:S(2)}) async-start(), calls=%async_computation.3 | async-start | bytes 10444800 | tf_op jit(solution)/shard_map/all_gather | solution.py:271
  17.4 7.6 %copy-start.71 = (s32[1,512]{1,0:T(1,128)S(1)}, s32[1,512]{1,0:T(1,128)}, u32[]{:S(2)}) copy-start(s32[1,512]{1,0:T(1,128)} %param.22) | copy-start | bytes 6148
  17.4 7.6 %copy-start.66 = (s32[1,512]{1,0:T(1,128)S(1)}, s32[1,512]{1,0:T(1,128)}, u32[]{:S(2)}) copy-start(s32[1,512]{1,0:T(1,128)} %param.21) | copy-start | bytes 6148
  19.2 144.5 %all-gather.5.cloned.1.call-start = ((), (), s32[]{:S(2)}) async-start(), calls=%async_computation.4 | async-start | bytes 1671168 | tf_op jit(solution)/shard_map/all_gather | solution.py:272
  19.2 13.0 %collective-permute-start = (bf16[256,768]{1,0:T(8,128)(2,1)S(1)}, bf16[256,768]{1,0:T(8,128)(2,1)S(1)}, u32[]{:S(2)}, u32[]{:S(2)}) collective-permute-start(bf16[256,768]{1,0:T(8,128)(2,1)S(1)} %bitcast.42), channel_id=1, source_target_pairs={{0,1},{1,0},{2,3},{3,2},{4,5},{5,4},{6,7},{7,6},{8,9},{9,8},{10,11... | collective-permute-start | bytes 1179656 | tf_op jit(solution)/shard_map/ppermute | solution.py:31
  22.2 18.5 %collective-permute-start.5 = (bf16[256,768]{1,0:T(8,128)(2,1)S(1)}, bf16[256,768]{1,0:T(8,128)(2,1)}, u32[]{:S(2)}, u32[]{:S(2)}) collective-permute-start(bf16[256,768]{1,0:T(8,128)(2,1)S(1)} %bitcast.41), channel_id=1, source_target_pairs={{0,1},{1,0},{2,3},{3,2},{4,5},{5,4},{6,7},{7,6},{8,9},{9,8},{10,11... | collective-permute-start | bytes 1179656 | tf_op jit(solution)/shard_map/ppermute | solution.py:31
  22.3 98.0 %collective-permute-start.2 = (bf16[1024,768]{1,0:T(8,128)(2,1)}, bf16[1024,768]{1,0:T(8,128)(2,1)}, u32[]{:S(2)}, u32[]{:S(2)}) collective-permute-start(bf16[1024,768]{1,0:T(8,128)(2,1)} %bitcast.47), channel_id=1, source_target_pairs={{0,1},{1,0},{2,3},{3,2},{4,5},{5,4},{6,7},{7,6},{8,9},{9,8},{10,11... | collective-permute-start | bytes 4718600 | tf_op jit(solution)/shard_map/ppermute | solution.py:31
  24.9 317.5 %reduce-scatter.8.cloned.1.call-start = ((), (), s32[]{:S(2)}) async-start(), calls=%async_computation.7 | async-start | bytes 1671168 | tf_op jit(solution)/shard_map/reduce_scatter | solution.py:341
  42.7 67.1 %copy-start.31 = (bf16[256,768]{1,0:T(8,128)(2,1)}, bf16[256,768]{1,0:T(8,128)(2,1)S(1)}, u32[]{:S(2)}) copy-start(bf16[256,768]{1,0:T(8,128)(2,1)S(1)} %get-tuple-element.109) | copy-start | bytes 1179652
  42.7 138.4 %copy-start.29 = (bf16[256,768]{1,0:T(8,128)(2,1)}, bf16[256,768]{1,0:T(8,128)(2,1)S(1)}, u32[]{:S(2)}) copy-start(bf16[256,768]{1,0:T(8,128)(2,1)S(1)} %get-tuple-element.108) | copy-start | bytes 1179652
  43.0 66.9 %copy-start.67 = (f32[512]{0:T(512)}, f32[512]{0:T(512)S(1)}, u32[]{:S(2)}) copy-start(f32[512]{0:T(512)S(1)} %add_rsqrt_fusion.2) | copy-start | bytes 6148
  107.0 13.4 %copy-start.46 = (bf16[768,6400]{1,0:T(8,128)(2,1)S(1)}, bf16[768,6400]{1,0:T(8,128)(2,1)}, u32[]{:S(2)}) copy-start(bf16[768,6400]{1,0:T(8,128)(2,1)} %all-gather.3.cloned.1.call-done) | copy-start | bytes 29491204
  110.0 6.3 %copy-start.8 = (bf16[512,384]{1,0:T(8,128)(2,1)}, bf16[512,384]{1,0:T(8,128)(2,1)S(1)}, u32[]{:S(2)}) copy-start(bf16[512,384]{1,0:T(8,128)(2,1)S(1)} %get-tuple-element.65.k_ref) | copy-start | bytes 1179652
  110.0 6.3 %copy-start.10 = (bf16[512,384]{1,0:T(8,128)(2,1)}, bf16[512,384]{1,0:T(8,128)(2,1)S(1)}, u32[]{:S(2)}) copy-start(bf16[512,384]{1,0:T(8,128)(2,1)S(1)} %get-tuple-element.66.q_ref) | copy-start | bytes 1179652
  110.0 10.3 %copy-start.73 = (bf16[1,1024,768]{2,1,0:T(8,128)(2,1)S(1)}, bf16[1,1024,768]{2,1,0:T(8,128)(2,1)}, u32[]{:S(2)}) copy-start(bf16[1,1024,768]{2,1,0:T(8,128)(2,1)} %param.20) | copy-start | bytes 4718596
  118.9 11.3 %copy-start.12 = (bf16[512,384]{1,0:T(8,128)(2,1)}, bf16[512,384]{1,0:T(8,128)(2,1)S(1)}, u32[]{:S(2)}) copy-start(bf16[512,384]{1,0:T(8,128)(2,1)S(1)} %get-tuple-element.29.o_ref) | copy-start | bytes 1179652
  118.9 11.3 %collective-permute-start.1 = (bf16[512,384]{1,0:T(8,128)(2,1)S(1)}, bf16[512,384]{1,0:T(8,128)(2,1)S(1)}, u32[]{:S(2)}, u32[]{:S(2)}) collective-permute-start(bf16[512,384]{1,0:T(8,128)(2,1)S(1)} %get-tuple-element.29.o_ref), channel_id=1, source_target_pairs={{0,1},{1,0},{2,3},{3,2},{4,5},{5,4},{6,7},{7,6},{8,9},{9,8},{10,11... | collective-permute-start | bytes 1179656 | tf_op jit(solution)/shard_map/ppermute | solution.py:31
  124.7 7.1 %copy-start.2 = (bf16[2048,384]{1,0:T(8,128)(2,1)}, bf16[2048,384]{1,0:T(8,128)(2,1)S(1)}, u32[]{:S(2)}) copy-start(bf16[2048,384]{1,0:T(8,128)(2,1)S(1)} %get-tuple-element.62.v_ref) | copy-start | bytes 4718596
  124.7 7.1 %copy-start.4 = (bf16[2048,384]{1,0:T(8,128)(2,1)}, bf16[2048,384]{1,0:T(8,128)(2,1)S(1)}, u32[]{:S(2)}) copy-start(bf16[2048,384]{1,0:T(8,128)(2,1)S(1)} %get-tuple-element.63.k_ref) | copy-start | bytes 4718596
  124.7 5.5 %copy-start.32 = (bf16[256,768]{1,0:T(8,128)(2,1)S(1)}, bf16[256,768]{1,0:T(8,128)(2,1)}, u32[]{:S(2)}) copy-start(bf16[256,768]{1,0:T(8,128)(2,1)} %copy-done.31) | copy-start | bytes 1179652
  131.2 26.6 %copy-start.20 = (f32[512,768]{1,0:T(8,128)}, f32[512,768]{1,0:T(8,128)S(1)}, u32[]{:S(2)}) copy-start(f32[512,768]{1,0:T(8,128)S(1)} %get-tuple-element.102) | copy-start | bytes 4718596
  131.8 15.4 %copy-start.16 = (bf16[512,384]{1,0:T(8,128)(2,1)}, bf16[512,384]{1,0:T(8,128)(2,1)S(1)}, u32[]{:S(2)}) copy-start(bf16[512,384]{1,0:T(8,128)(2,1)S(1)} %convolution_convert_fusion.11.q_ref) | copy-start | bytes 1179652
  147.2 11.4 %copy-start.14 = (bf16[512,384]{1,0:T(8,128)(2,1)}, bf16[512,384]{1,0:T(8,128)(2,1)S(1)}, u32[]{:S(2)}) copy-start(bf16[512,384]{1,0:T(8,128)(2,1)S(1)} %get-tuple-element.30.o_ref) | copy-start | bytes 1179652
  147.2 10.4 %collective-permute-start.3 = (bf16[512,384]{1,0:T(8,128)(2,1)S(1)}, bf16[512,384]{1,0:T(8,128)(2,1)S(1)}, u32[]{:S(2)}, u32[]{:S(2)}) collective-permute-start(bf16[512,384]{1,0:T(8,128)(2,1)S(1)} %get-tuple-element.30.o_ref), channel_id=1, source_target_pairs={{0,1},{1,0},{2,3},{3,2},{4,5},{5,4},{6,7},{7,6},{8,9},{9,8},{10,11... | collective-permute-start | bytes 1179656 | tf_op jit(solution)/shard_map/ppermute | solution.py:31
  158.7 39.3 %copy-start.63 = (f32[512]{0:T(512)}, f32[512]{0:T(512)S(1)}, u32[]{:S(2)}) copy-start(f32[512]{0:T(512)S(1)} %add_rsqrt_fusion) | copy-start | bytes 6148
  172.5 175.8 %reduce-scatter.6.cloned.1.call-start = ((), (), s32[]{:S(2)}) async-start(), calls=%async_computation.6 | async-start | bytes 3342336 | tf_op jit(solution)/shard_map/reduce_scatter | solution.py:338
  174.2 6.9 %copy-start.33 = (bf16[256,768]{1,0:T(8,128)(2,1)S(1)}, bf16[256,768]{1,0:T(8,128)(2,1)}, u32[]{:S(2)}) copy-start(bf16[256,768]{1,0:T(8,128)(2,1)} %copy-done.31) | copy-start | bytes 1179652
  179.7 18.3 %collective-permute-start.6 = (bf16[512,768]{1,0:T(8,128)(2,1)}, bf16[512,768]{1,0:T(8,128)(2,1)}, u32[]{:S(2)}, u32[]{:S(2)}) collective-permute-start(bf16[512,768]{1,0:T(8,128)(2,1)} %get-tuple-element.105), channel_id=1, source_target_pairs={{0,1},{1,0},{2,3},{3,2},{4,5},{5,4},{6,7},{7,6},{8,9},{9,8},{10,11... | collective-permute-start | bytes 2359304 | tf_op jit(solution)/shard_map/ppermute | solution.py:31
  189.6 188.5 %reduce-scatter.4.cloned.1.call-start = ((), (), s32[]{:S(2)}) async-start(), calls=%async_computation.5 | async-start | bytes 5222400 | tf_op jit(solution)/shard_map/reduce_scatter | solution.py:372
  205.9 33.3 %copy-start.21 = (f32[512,768]{1,0:T(8,128)S(1)}, f32[512,768]{1,0:T(8,128)}, u32[]{:S(2)}) copy-start(f32[512,768]{1,0:T(8,128)} %copy-done.20) | copy-start | bytes 4718596
  237.7 22.8 %collective-permute-start.7 = (bf16[512,384]{1,0:T(8,128)(2,1)}, bf16[512,384]{1,0:T(8,128)(2,1)}, u32[]{:S(2)}, u32[]{:S(2)}) collective-permute-start(bf16[512,384]{1,0:T(8,128)(2,1)} %get-tuple-element.33), channel_id=1, source_target_pairs={{0,1},{1,0},{2,3},{3,2},{4,5},{5,4},{6,7},{7,6},{8,9},{9,8},{10,11... | collective-permute-start | bytes 1179656 | tf_op jit(solution)/shard_map/ppermute | solution.py:31
  284.6 8.4 %copy-start.38 = (f32[512,768]{1,0:T(8,128)}, f32[512,768]{1,0:T(8,128)S(1)}, u32[]{:S(2)}) copy-start(f32[512,768]{1,0:T(8,128)S(1)} %fusion.19) | copy-start | bytes 4718596
  284.7 8.2 %collective-permute-start.8 = (bf16[256,768]{1,0:T(8,128)(2,1)S(1)}, bf16[256,768]{1,0:T(8,128)(2,1)S(1)}, u32[]{:S(2)}, u32[]{:S(2)}) collective-permute-start(bf16[256,768]{1,0:T(8,128)(2,1)S(1)} %dynamic-slice_convert_fusion), channel_id=1, source_target_pairs={{0,1},{1,0},{2,3},{3,2},{4,5},{5,4},{6,7},{7,6},{8,9},{9,8},{10,11... | collective-permute-start | bytes 1179656 | tf_op jit(solution)/shard_map/ppermute | solution.py:31
  286.3 6.6 %copy-start.26 = (f32[512,768]{1,0:T(8,128)S(1)}, f32[512,768]{1,0:T(8,128)}, u32[]{:S(2)}) copy-start(f32[512,768]{1,0:T(8,128)} %fusion.67) | copy-start | bytes 4718596
  286.4 6.6 %copy-start.64 = (f32[256]{0:T(256)S(1)}, f32[256]{0:T(256)}, u32[]{:S(2)}) copy-start(f32[256]{0:T(256)} %dynamic-slice.3) | copy-start | bytes 3076
  294.4 5.0 %copy-start.75 = (bf16[1024,768]{1,0:T(8,128)(2,1)S(1)}, bf16[1024,768]{1,0:T(8,128)(2,1)}, u32[]{:S(2)}) copy-start(bf16[1024,768]{1,0:T(8,128)(2,1)} %all-gather.5.cloned.1.call-done) | copy-start | bytes 4718596
  294.4 5.0 %copy-start.77 = (bf16[512,1024]{1,0:T(8,128)(2,1)S(1)}, bf16[512,1024]{1,0:T(8,128)(2,1)}, u32[]{:S(2)}) copy-start(bf16[512,1024]{1,0:T(8,128)(2,1)} %copy-done.76) | copy-start | bytes 3145732
  299.1 41.3 %copy-start.25 = (f32[512,768]{1,0:T(8,128)S(1)}, f32[512,768]{1,0:T(8,128)}, u32[]{:S(2)}) copy-start(f32[512,768]{1,0:T(8,128)} %copy-done.23) | copy-start | bytes 4718596
  299.1 43.9 %collective-permute-start.9 = (bf16[1024,768]{1,0:T(8,128)(2,1)}, bf16[1024,768]{1,0:T(8,128)(2,1)}, u32[]{:S(2)}, u32[]{:S(2)}) collective-permute-start(bf16[1024,768]{1,0:T(8,128)(2,1)} %convolution_convert_fusion.5), channel_id=1, source_target_pairs={{0,1},{1,0},{2,3},{3,2},{4,5},{5,4},{6,7},{7,6},{8,9},{9,8},{10,11... | collective-permute-start | bytes 4718600 | tf_op jit(solution)/shard_map/ppermute | solution.py:31
  300.4 40.8 %copy-start.39 = (f32[512,768]{1,0:T(8,128)S(1)}, f32[512,768]{1,0:T(8,128)}, u32[]{:S(2)}) copy-start(f32[512,768]{1,0:T(8,128)} %copy-done.38) | copy-start | bytes 4718596
  300.5 39.9 %collective-permute-start.4 = (bf16[256,768]{1,0:T(8,128)(2,1)S(1)}, bf16[256,768]{1,0:T(8,128)(2,1)S(1)}, u32[]{:S(2)}, u32[]{:S(2)}) collective-permute-start(bf16[256,768]{1,0:T(8,128)(2,1)S(1)} %dynamic-slice_convert_fusion.1), channel_id=1, source_target_pairs={{0,1},{1,0},{2,3},{3,2},{4,5},{5,4},{6,7},{7,6},{8,9},{9,8},{10,11... | collective-permute-start | bytes 1179656 | tf_op jit(solution)/shard_map/ppermute | solution.py:31
  342.4 7.4 %copy-start.61 = (bf16[64,768]{1,0:T(8,128)(2,1)S(1)}, bf16[64,768]{1,0:T(8,128)(2,1)}, u32[]{:S(2)}) copy-start(bf16[64,768]{1,0:T(8,128)(2,1)} %reduce-scatter.8.cloned.1.call-done) | copy-start | bytes 294916
  342.4 7.4 %collective-permute-start.12 = (bf16[64,768]{1,0:T(8,128)(2,1)}, bf16[64,768]{1,0:T(8,128)(2,1)S(1)}, u32[]{:S(2)}, u32[]{:S(2)}) collective-permute-start(bf16[64,768]{1,0:T(8,128)(2,1)} %reduce-scatter.8.cloned.1.call-done), channel_id=1, source_target_pairs={{0,1},{1,0},{2,3},{3,2},{4,5},{5,4},{6,7},{7,6},{8,9},{9,8},{10,11... | collective-permute-start | bytes 294920 | tf_op jit(solution)/shard_map/ppermute | solution.py:31
  348.3 5.9 %collective-permute-start.11 = (bf16[48,2048]{1,0:T(8,128)(2,1)}, bf16[48,2048]{1,0:T(8,128)(2,1)S(1)}, u32[]{:S(2)}, u32[]{:S(2)}) collective-permute-start(bf16[48,2048]{1,0:T(8,128)(2,1)} %reduce-scatter.6.cloned.1.call-done), channel_id=1, source_target_pairs={{0,1},{1,0},{2,3},{3,2},{4,5},{5,4},{6,7},{7,6},{8,9},{9,8},{10,11... | collective-permute-start | bytes 589832 | tf_op jit(solution)/shard_map/ppermute | solution.py:31
  378.1 7.5 %collective-permute-start.10 = (bf16[48,3200]{1,0:T(8,128)(2,1)}, bf16[48,3200]{1,0:T(8,128)(2,1)S(1)}, u32[]{:S(2)}, u32[]{:S(2)}) collective-permute-start(bf16[48,3200]{1,0:T(8,128)(2,1)} %reduce-scatter.4.cloned.1.call-done), channel_id=1, source_target_pairs={{0,1},{1,0},{2,3},{3,2},{4,5},{5,4},{6,7},{7,6},{8,9},{9,8},{10,11... | collective-permute-start | bytes 921608 | tf_op jit(solution)/shard_map/ppermute | solution.py:31
  381.8 10.0 %copy-start.1 = (bf16[128,768]{1,0:T(8,128)(2,1)S(1)}, bf16[128,768]{1,0:T(8,128)(2,1)}, u32[]{:S(2)}) copy-start(bf16[128,768]{1,0:T(8,128)(2,1)} %param.37) | copy-start | bytes 589828
  (51 other events, 112.6 us)
Sparse Core Ops, SparseCore 0:
  19.3 86.0 all-gather.2
  108.3 37.9 all-gather.4
  172.6 57.8 reduce-scatter.7
  234.2 65.3 reduce-scatter.5
  303.4 74.6 reduce-scatter.3
